TPU v7x, 32 devices: a whole 2x2x4 slice. The times are simulated.
32 devices in a mesh: runs: 2 (over y), gx: 4 (over z), gy: 2 (over x), gz: 2 (over core).
Axes of the slice: x: 2, y: 2, z: 4, core: 2. Of those that a mesh axis runs over, the one named last changes fastest.
Arguments:
- offsets: float32 [3, 32768], P(None, ('runs', 'gx', 'gy', 'gz')), parts along dimension 1, may hold values from -0.5 to 0.5
- particle_mass: float32 [32768], P(('runs', 'gx', 'gy', 'gz')), parts along dimension 0, may hold values from 0.5 to 2
- velocity: float32 [3, 32768], P(None, ('runs', 'gx', 'gy', 'gz')), parts along dimension 1, may hold values from -6 to 6
- home_cell: int32 [32768], P(('runs', 'gx', 'gy', 'gz')), parts along dimension 0, may hold values from 0 to 4095
- home_tile: int32 [32768], P(('runs', 'gx', 'gy', 'gz')), parts along dimension 0, may hold values from 0 to 7, as said below
- conv1_weight: bfloat16 [16, 4, 3, 3, 3], replicated, may hold values from -2.5 to 2.5
- conv1_bias: float32 [16], replicated, may hold values from -3 to 3
- conv2_weight: bfloat16 [16, 16, 3, 3, 3], replicated, may hold values from -0.3125 to 0.3125
- conv2_bias: float32 [16], replicated, may hold values from -3 to 3
- head_weight: bfloat16 [3, 16], replicated, may hold values from -1.5 to 1.5
Outputs:
- forces: float32 [3, 32768], P(None, ('runs', 'gx', 'gy', 'gz')), parts along dimension 1
There are 2 independent parts, one for each index of `runs`. A program takes and returns all parts, laid end to end along the dimension named above; an argument that names none is the same for every part. Nothing has to cross between parts.
Inputs may be any that keep to these rules, and one draw needn't show every extreme that they name: `home_tile`: within the rows of one device (aligned blocks of 1024 rows) no tile is named more than 256 times; in every draw one tile is named exactly 256 times in every block.
All inputs are finite; a program needn't handle non-finite values.
Results may differ from a plain program's by a relative error of at most 0.0057.
Values may be sent and summed in bfloat16 or wider, within the bound.
No kernel may reach another device: no remote copies, remote signals or barrier semaphores. Data moves between devices by JAX's collectives and lax.ppermute only.
A program may use at most 64 MiB of HBM per device.

v0:
```python
import jax
import jax.numpy as jnp
from jax import lax
from jax.sharding import PartitionSpec as P

TX = 16
TY = 128
TZ = 2


def padded(block, sides, width):
    for axis, dim in sides:
        count = lax.axis_size(axis)
        forward = [(i, i + 1) for i in range(count - 1)]
        forward.append((count - 1, 0))
        backward = [(target, source) for source, target in forward]
        low = lax.ppermute(
            lax.slice_in_dim(block, block.shape[dim] - width, None, axis=dim), axis, forward
        )
        high = lax.ppermute(lax.slice_in_dim(block, 0, width, axis=dim), axis, backward)
        block = jnp.concatenate([low, block, high], axis=dim)
    return block


def clear_planes(widened, rim_depth):
    gz_level = lax.axis_index("gz")
    last_level = lax.axis_size("gz") - 1
    extent = widened.shape[1]
    plane_index = lax.broadcasted_iota(jnp.int32, (1, extent, 1, 1), 1)
    outside = (plane_index < rim_depth) & (gz_level == 0) | (plane_index >= extent - rim_depth) & (
        gz_level == last_level
    )
    return jnp.where(outside, jnp.zeros((), widened.dtype), widened)


def extend(mesh_field):
    widened = padded(mesh_field, (("gx", 2), ("gy", 3), ("gz", 1)), 1)
    return clear_planes(widened, 1)


def convolve(widened, weight, bias_vec):
    summed = lax.conv_general_dilated(
        widened[None],
        weight,
        (1, 1, 1),
        "VALID",
        dimension_numbers=("NCDHW", "OIDHW", "NCDHW"),
        preferred_element_type=jnp.float32,
    )[0]
    return jax.nn.silu(summed + bias_vec[:, None, None, None]).astype(jnp.bfloat16)


def fold_edges(widened, axis_dim, keep_low, keep_high):
    extent = widened.shape[axis_dim]
    inner_part = lax.slice_in_dim(widened, 2, extent - 2, axis=axis_dim)
    low_rim = lax.slice_in_dim(widened, 0, 1, axis=axis_dim) * keep_low
    high_rim = lax.slice_in_dim(widened, extent - 1, extent, axis=axis_dim) * keep_high
    inner_count = extent - 4
    head_part = lax.slice_in_dim(inner_part, 0, 1, axis=axis_dim) + low_rim
    tail_part = lax.slice_in_dim(inner_part, inner_count - 1, inner_count, axis=axis_dim) + high_rim
    middle = lax.slice_in_dim(inner_part, 1, inner_count - 1, axis=axis_dim)
    return jnp.concatenate([head_part, middle, tail_part], axis=axis_dim)


def axis_pair(base, fraction):
    step_dir = jnp.where(fraction >= 0.0, 1, -1).astype(jnp.int32)
    return ((base, base + step_dir), (1.0 - jnp.abs(fraction), jnp.abs(fraction)))


def corner_table(cell_index, fractions):
    local_z = cell_index // (TX * TY) + 1
    local_x = cell_index // TY % TX + 1
    local_y = cell_index % TY + 1
    z_pair, z_weight = axis_pair(local_z, fractions[0])
    x_pair, x_weight = axis_pair(local_x, fractions[1])
    y_pair, y_weight = axis_pair(local_y, fractions[2])
    flat_list = []
    weight_list = []
    for pick_z in range(2):
        for pick_x in range(2):
            for pick_y in range(2):
                flat_list.append(
                    (z_pair[pick_z] * (TX + 2) + x_pair[pick_x]) * (TY + 2) + y_pair[pick_y]
                )
                weight_list.append(z_weight[pick_z] * x_weight[pick_x] * y_weight[pick_y])
    return (jnp.stack(flat_list), jnp.stack(weight_list))


def sample(widened, flat_index, weights):
    channels = widened.shape[0]
    picked = jnp.take(widened.reshape(channels, -1), flat_index.reshape(-1), axis=1).reshape(
        channels, 8, -1
    )
    return jnp.sum(picked * weights[None], axis=1)


def on_device(
    offsets,
    particle_mass,
    velocity,
    home_cell,
    home_tile,
    conv1_weight,
    conv1_bias,
    conv2_weight,
    conv2_bias,
    head_weight,
):
    local_rows = home_tile.shape[0]
    tile_count = lax.axis_size("gx") * lax.axis_size("gy")
    capacity = 2 * local_rows // tile_count
    tile_ids = jnp.arange(tile_count, dtype=jnp.int32)
    counts = jnp.sum((home_tile[:, None] == tile_ids[None, :]).astype(jnp.int32), axis=0)
    starts = jnp.cumsum(counts) - counts
    ordering = jnp.argsort(home_tile, stable=True)
    sorted_tile = home_tile[ordering]
    group_start = jnp.sum(
        jnp.where(sorted_tile[:, None] == tile_ids[None, :], starts[None, :], 0), axis=1
    )
    slot_sorted = sorted_tile * capacity + jnp.arange(local_rows, dtype=jnp.int32) - group_start
    slot_index = jnp.zeros((local_rows,), jnp.int32).at[ordering].set(slot_sorted)
    row_data = jnp.concatenate([offsets, particle_mass[None], velocity], axis=0)
    send_rows = jnp.zeros((7, tile_count * capacity), jnp.float32).at[:, slot_index].set(row_data)
    send_cells = (
        jnp.zeros((1, tile_count * capacity), jnp.int32).at[:, slot_index].set(home_cell[None])
    )
    got_rows, got_cells = (
        lax.all_to_all(send_rows, ("gx", "gy"), split_axis=1, concat_axis=1, tiled=True),
        lax.all_to_all(send_cells, ("gx", "gy"), split_axis=1, concat_axis=1, tiled=True),
    )
    flat_index, weights = corner_table(got_cells[0], got_rows[0:3])
    mass_row = got_rows[3:4]
    paint_values = jnp.concatenate([mass_row, mass_row * got_rows[4:7]], axis=0)
    contrib = (paint_values[:, None, :] * weights[None]).reshape(paint_values.shape[0], -1)
    extent_cells = (TZ + 2) * (TX + 2) * (TY + 2)
    painted = (
        jnp.zeros((paint_values.shape[0], extent_cells), jnp.float32)
        .at[:, flat_index.reshape(-1)]
        .add(contrib)
    )
    painted = painted.reshape(paint_values.shape[0], TZ + 2, TX + 2, TY + 2)
    widened = padded(painted, (("gx", 2), ("gy", 3), ("gz", 1)), 1)
    keep_low = (lax.axis_index("gz") > 0).astype(jnp.float32)
    keep_high = (lax.axis_index("gz") < lax.axis_size("gz") - 1).astype(jnp.float32)
    folded = fold_edges(widened, 2, 1.0, 1.0)
    folded = fold_edges(folded, 3, 1.0, 1.0)
    folded = fold_edges(folded, 1, keep_low, keep_high)
    density = folded.astype(jnp.bfloat16)
    deep_field = padded(density, (("gx", 2), ("gy", 3), ("gz", 1)), 2)
    deep_field = clear_planes(deep_field, 2)
    hidden = clear_planes(convolve(deep_field, conv1_weight, conv1_bias), 1)
    features = convolve(hidden, conv2_weight, conv2_bias)
    sampled = sample(extend(features), flat_index, weights)
    returned = lax.all_to_all(sampled, ("gx", "gy"), split_axis=1, concat_axis=1, tiled=True)
    forces = jnp.dot(
        head_weight.astype(jnp.float32), returned[:, slot_index], precision=lax.Precision.HIGHEST
    )
    return forces


def solution(mesh):
    in_specs = (
        P(None, ("runs", "gx", "gy", "gz")),
        P(("runs", "gx", "gy", "gz")),
        P(None, ("runs", "gx", "gy", "gz")),
        P(("runs", "gx", "gy", "gz")),
        P(("runs", "gx", "gy", "gz")),
        P(),
        P(),
        P(),
        P(),
        P(),
    )
    out_specs = P(None, ("runs", "gx", "gy", "gz"))
    return jax.shard_map(
        on_device, mesh=mesh, in_specs=in_specs, out_specs=out_specs, check_vma=False
    )
```

profile of v0, /device:TPU:0, one launch (start us, length us, event | category | flops | bytes accessed | tf_op | source)
XLA Modules:
  0.0 315.5 jit_solution(11728118892970297130)
XLA Ops:
  0.0 0.9 convert_reduce_fusion
  0.9 5.1 %sort.17 = (s32[1024]{0:T(1024)}, s32[1024]{0:T(1024)S(1)}) sort(s32[1024]{0:T(1024)} %param.14, s32[1024]{0:T(1024)S(1)} %iota.29), dimensions={0}, to_apply=%region_0.0 | sort | flops 10240 | bytes 16384 | tf_op jit(solution)/shard_map/jit(argsort)/sort | solution.py:115
  6.0 4.5 %gather_fusion = s32[1024]{0:T(1024)S(1)} fusion(s32[1024]{0:T(1024)S(1)} %copy-done.1, s32[1024]{0:T(1024)S(1)} %get-tuple-element.61), kind=kCustom, calls=%fused_computation | custom fusion | bytes 12288 | tf_op jit(solution)/shard_map/gather | solution.py:116
  10.8 4.3 %scatter_custom_fusion = s32[1024]{0:T(1024)S(1)} fusion(s32[1024]{0:T(1024)S(1)} %get-tuple-element.62, s32[1024]{0:T(1024)S(1)} %add_subtract_fusion, s32[]{:T(128)} %constant.85.clone.1), kind=kCustom, calls=%fused_computation.117 | custom fusion | bytes 4100 | tf_op jit(solution)/shard_map/scatter | solution.py:121
  15.2 0.2 copy.62
  15.4 3.3 %scatter_custom_fusion.2 = f32[7,2048]{0,1:T(8,128)S(1)} fusion(s32[1024]{0:T(1024)S(1)} %get-tuple-element.60, f32[1024,7]{1,0:T(8,128)S(1)} %copy.62, f32[]{:T(128)} %constant.100.clone.1), kind=kCustom, calls=%fused_computation.36 | custom fusion | bytes 57348 | tf_op jit(solution)/shard_map/scatter | solution.py:123
  18.7 1.0 copy.63
  19.7 7.3 %all-to-all-start.1 = ((f32[7,8,256]{2,0,1:T(8,128)}), f32[7,8,256]{2,0,1:T(8,128)S(1)}, u32[]{:S(2)}, u32[]{:S(2)}) async-start(f32[7,8,256]{2,0,1:T(8,128)} %copy.63), calls=%async_computation.1 | async-start | bytes 131072 | tf_op jit(solution)/shard_map/all_to_all | solution.py:128
  27.0 5.0 %scatter_custom_fusion.1 = s32[2048]{0:T(1024)} fusion(s32[1024]{0:T(1024)S(1)} %get-tuple-element.60, s32[1024]{0:T(1024)} %param.13, s32[]{:T(128)} %constant.85.clone.1), kind=kCustom, calls=%fused_computation.110 | custom fusion | bytes 8704 | tf_op jit(solution)/shard_map/scatter | solution.py:125
  32.0 1.9 all-to-all-done.1
  33.9 4.1 %all-to-all-start = ((s32[1,8,256]{2,0,1:T(1,128)}), s32[1,8,256]{2,0,1:T(1,128)S(1)}, u32[]{:S(2)}, u32[]{:S(2)}) async-start(s32[1,8,256]{2,0,1:T(1,128)} %bitcast.2), calls=%async_computation | async-start | bytes 16384 | tf_op jit(solution)/shard_map/all_to_all | solution.py:129
  38.4 0.4 copy.64
  38.7 5.8 %all-to-all-done = s32[1,8,256]{2,0,1:T(1,128)S(1)} async-done(((s32[1,8,256]{2,0,1:T(1,128)}), s32[1,8,256]{2,0,1:T(1,128)S(1)}, u32[]{:S(2)}, u32[]{:S(2)}) %all-to-all-start) | async-done | bytes 8224 | tf_op jit(solution)/shard_map/all_to_all | solution.py:129
  45.0 4.6 %bitcast_multiply_fusion = f32[4,16384]{0,1:T(8,128)} fusion(f32[16384]{0:T(1024)S(1)} %bitcast.77, f32[4,2048]{0,1:T(8,128)S(1)} %copy.64), kind=kLoop, calls=%fused_computation.9 | loop fusion | flops 65536 | bytes 360448 | tf_op jit(solution)/shard_map/mul | solution.py:134
  49.6 100.7 %scatter_custom_fusion.3 = f32[4,9360]{0,1:T(8,128)} fusion(s32[16384]{0:T(1024)S(1)} %bitcast.78, f32[4,16384]{0,1:T(8,128)} %bitcast_multiply_fusion, f32[]{:T(128)} %constant.100.clone.1), kind=kCustom, calls=%fused_computation.7 | custom fusion | flops 65536 | bytes 411908 | tf_op jit(solution)/shard_map/scatter-add | solution.py:139
  150.3 3.1 copy.65
  153.4 0.4 reshape.726
  153.8 1.2 collective-permute-start
  155.0 2.7 collective-permute-start.1
  157.7 1.7 collective-permute-done
  159.6 0.9 collective-permute-start.2
  160.5 1.2 collective-permute-start.3
  161.7 4.2 %collective-permute-done.2 = f32[4,4,20,1]{3,2,1,0:T(8,128)S(1)} collective-permute-done((f32[4,4,20,1]{3,2,1,0:T(8,128)S(1)}, f32[4,4,20,1]{3,2,1,0:T(8,128)S(1)}, u32[]{:S(2)}, u32[]{:S(2)}) %collective-permute-start.2) | collective-permute-done | bytes 1312 | tf_op jit(solution)/shard_map/ppermute | solution.py:17
  165.9 2.1 collective-permute-done.3
  168.3 0.5 collective-permute-start.5
  168.8 0.8 collective-permute-done.4
  169.7 0.3 pad_maximum_fusion
  170.1 0.2 maximum_add_fusion.1
  170.3 0.2 maximum_add_fusion
  170.7 0.2 slice_add_fusion.1
  171.2 3.9 %collective-permute-start.7 = (bf16[4,2,2,128]{3,2,1,0:T(2,128)(2,1)S(1)}, bf16[4,2,2,128]{3,2,1,0:T(2,128)(2,1)S(1)}, u32[]{:S(2)}, u32[]{:S(2)}) collective-permute-start(bf16[4,2,2,128]{3,2,1,0:T(2,128)(2,1)S(1)} %get-tuple-element.43), channel_id=1, source_target_pairs={{4,0},{8,4},{12,8},{0,12},{5,1},{9,5},{13,9},{1,13},{6,2},{10,6},{... | collective-permute-start | bytes 12296 | tf_op jit(solution)/shard_map/ppermute | solution.py:20
  175.1 1.5 collective-permute-done.6
  176.7 1.0 collective-permute-start.8
  177.8 1.1 collective-permute-start.9
  178.8 2.1 collective-permute-done.8
  180.9 1.0 collective-permute-done.9
  182.1 0.5 collective-permute-start.11
  182.7 0.7 collective-permute-done.10
  183.7 0.7 reshape.806
  184.5 3.3 %copy.68 = bf16[4,6,20,1,8,17]{4,0,5,2,1,3:T(4,128)(2,1)S(1)} copy(bf16[4,6,20,1,8,17]{5,4,2,1,0,3:T(8,128)(2,1)S(1)} %reshape.806) | data formatting | bytes 261120 | tf_op jit(solution)/shard_map/conv_general_dilated | solution.py:42
  188.0 12.3 %select_bitcast_fusion = bf16[4,18,1,8,17,16]{5,3,4,1,0,2:T(8,128)(2,1)S(1)} fusion(f32[16]{0:T(128)S(1)} %copy-done.8, pred[4]{0:T(512)(128)(4,1)S(1)} %and_or_fusion.1, pred[8,17]{0,1:T(8,128)(4,1)S(1)} %copy-done.9, bf16[16,4,3,3,3]{0,1,4,3,2:T(4,128)(2,1)S(1)} %copy-done.7, bf16[4,6,20,1,7,2]{4,0,5,2,1,3:T(4,128)(2,1)S(1)} %slice.192, ...), kind=kOutput, calls=%fused_computation.22 | convolution fusion | flops 35688960 | bytes 461004 | tf_op jit(solution)/shard_map/conv_general_dilated | solution.py:42
  200.4 4.5 %fusion.6 = f32[2,16,8,17,16]{4,2,3,1,0:T(8,128)} fusion(bf16[16,16,3,3,3]{1,0,4,3,2:T(8,128)(2,1)S(1)} %copy-done, bf16[4,18,1,7,2,16]{5,3,4,1,0,2:T(8,128)(2,1)S(1)} %slice.193, bf16[4,18,1,8,17,16]{5,3,4,1,0,2:T(8,128)(2,1)S(1)} %select_bitcast_fusion), kind=kOutput, calls=%fused_computation.18 | convolution fusion | flops 61212672 | bytes 637952 | tf_op jit(solution)/shard_map/conv_general_dilated | solution.py:42
  204.9 2.9 copy.69
  207.9 0.6 reshape.736
  208.6 0.9 collective-permute-start.12
  209.5 3.3 %collective-permute-start.13 = (bf16[16,2,1,128]{3,0,2,1:T(8,128)(2,1)S(1)}, bf16[16,2,1,128]{3,0,2,1:T(8,128)(2,1)S(1)}, u32[]{:S(2)}, u32[]{:S(2)}) collective-permute-start(bf16[16,2,1,128]{3,0,2,1:T(8,128)(2,1)S(1)} %get-tuple-element.32), channel_id=1, source_target_pairs={{4,0},{8,4},{12,8},{0,12},{5,1},{9,5},{13,9},{1,13},{6,2},{10,6},{... | collective-permute-start | bytes 24584 | tf_op jit(solution)/shard_map/ppermute | solution.py:20
  212.8 0.2 broadcast_in_dim.113
  213.1 1.1 collective-permute-done.12
  214.3 1.2 collective-permute-start.14
  215.5 0.9 collective-permute-start.15
  216.4 4.7 %collective-permute-done.14 = bf16[16,2,18,1]{3,0,2,1:T(8,128)(2,1)S(1)} collective-permute-done((bf16[16,2,18,1]{3,0,2,1:T(8,128)(2,1)S(1)}, bf16[16,2,18,1]{3,0,2,1:T(8,128)(2,1)S(1)}, u32[]{:S(2)}, u32[]{:S(2)}) %collective-permute-start.14) | collective-permute-done | bytes 1184 | tf_op jit(solution)/shard_map/ppermute | solution.py:17
  221.1 1.7 collective-permute-done.15
  223.1 0.5 collective-permute-start.17
  223.6 0.8 collective-permute-done.16
  225.1 0.7 concatenate.75
  225.8 1.9 copy.71
  227.7 6.2 %broadcast_select_fusion = bf16[16,9360]{0,1:T(8,128)(2,1)S(1)} fusion(bf16[16,9360]{0,1:T(8,128)(2,1)} %copy.71, pred[9360]{0:T(1024)(128)(4,1)S(1)} %broadcast_in_dim.113), kind=kLoop, calls=%fused_computation.24 | loop fusion | flops 149760 | bytes 608400 | tf_op jit(solution)/shard_map/jit(_where)/select_n | solution.py:33
  234.0 57.5 %gather_fusion.1 = bf16[16384,16]{1,0:T(8,128)(2,1)} fusion(bf16[16,9360]{0,1:T(8,128)(2,1)S(1)} %broadcast_select_fusion, s32[16384]{0:T(1024)S(1)} %broadcast_clamp_fusion), kind=kCustom, calls=%fused_computation.1 | custom fusion | bytes 1114112 | tf_op jit(solution)/shard_map/jit(_take)/gather | solution.py:91
  291.4 6.8 %multiply_reduce_fusion = f32[16,2048]{0,1:T(8,128)S(1)} fusion(f32[8,2048]{1,0:T(8,128)S(1)} %stack.5, bf16[16,8,2048]{0,2,1:T(8,128)(2,1)} %bitcast.71, pred[8,2048]{1,0:T(8,128)(4,1)S(1)} %compare_and_fusion), kind=kLoop, calls=%fused_computation.10 | loop fusion | flops 1015808 | bytes 737280 | tf_op jit(solution)/shard_map/reduce_sum | solution.py:94
  298.2 0.3 copy.73
  298.5 12.9 %all_to_all.33 = f32[16,8,256]{2,0,1:T(8,128)S(1)} all-to-all(f32[16,8,256]{2,0,1:T(8,128)S(1)} %copy.73), channel_id=1, replica_groups=mesh['runs'=2,'gx'=4,'gy'=2,'gz'=2] {'gx','gy'}, dimensions={1} | all-to-all | bytes 262144 | tf_op jit(solution)/shard_map/all_to_all | solution.py:154
  311.4 0.3 copy.74
  311.7 2.8 gather_fusion.2
  314.6 1.0 convolution_bitcast_fusion
  (82 shorter events, 4.5 us)
Async XLA Ops:
  0.0 200.4 %copy-start = (bf16[16,16,3,3,3]{1,0,4,3,2:T(8,128)(2,1)S(1)}, bf16[16,16,3,3,3]{1,0,4,3,2:T(8,128)(2,1)}, u32[]{:S(2)}) copy-start(bf16[16,16,3,3,3]{1,0,4,3,2:T(8,128)(2,1)} %param.17) | copy-start | bytes 41476
  0.0 5.9 %copy-start.1 = (s32[1024]{0:T(1024)S(1)}, s32[1024]{0:T(1024)}, u32[]{:S(2)}) copy-start(s32[1024]{0:T(1024)} %param.14) | copy-start | bytes 12292
  0.0 15.1 %copy-start.4 = (f32[1024]{0:T(1024)S(1)}, f32[1024]{0:T(1024)}, u32[]{:S(2)}) copy-start(f32[1024]{0:T(1024)} %param.11) | copy-start | bytes 12292
  0.0 15.1 %copy-start.3 = (f32[3,1024]{1,0:T(4,128)S(1)}, f32[3,1024]{1,0:T(4,128)}, u32[]{:S(2)}) copy-start(f32[3,1024]{1,0:T(4,128)} %param.10) | copy-start | bytes 36868
  0.0 15.1 %copy-start.2 = (f32[3,1024]{1,0:T(4,128)S(1)}, f32[3,1024]{1,0:T(4,128)}, u32[]{:S(2)}) copy-start(f32[3,1024]{1,0:T(4,128)} %param.12) | copy-start | bytes 36868
  19.7 14.2 %all-to-all-start.1 = ((f32[7,8,256]{2,0,1:T(8,128)}), f32[7,8,256]{2,0,1:T(8,128)S(1)}, u32[]{:S(2)}, u32[]{:S(2)}) async-start(f32[7,8,256]{2,0,1:T(8,128)} %copy.63), calls=%async_computation.1 | async-start | bytes 131072 | tf_op jit(solution)/shard_map/all_to_all | solution.py:128
  33.9 10.7 %all-to-all-start = ((s32[1,8,256]{2,0,1:T(1,128)}), s32[1,8,256]{2,0,1:T(1,128)S(1)}, u32[]{:S(2)}, u32[]{:S(2)}) async-start(s32[1,8,256]{2,0,1:T(1,128)} %bitcast.2), calls=%async_computation | async-start | bytes 16384 | tf_op jit(solution)/shard_map/all_to_all | solution.py:129
  153.8 5.6 %collective-permute-start = (f32[4,4,1,130]{3,2,1,0:T(1,128)S(1)}, f32[4,4,1,130]{3,2,1,0:T(1,128)S(1)}, u32[]{:S(2)}, u32[]{:S(2)}) collective-permute-start(f32[4,4,1,130]{3,2,1,0:T(1,128)S(1)} %get-tuple-element.25), channel_id=1, source_target_pairs={{0,4},{4,8},{8,12},{12,0},{1,5},{5,9},{9,13},{13,1},{2,6},{6,10},{... | collective-permute-start | bytes 24968 | tf_op jit(solution)/shard_map/ppermute | solution.py:17
  155.0 4.4 %collective-permute-start.1 = (f32[4,4,1,130]{3,2,1,0:T(1,128)S(1)}, f32[4,4,1,130]{3,2,1,0:T(1,128)S(1)}, u32[]{:S(2)}, u32[]{:S(2)}) collective-permute-start(f32[4,4,1,130]{3,2,1,0:T(1,128)S(1)} %get-tuple-element.26), channel_id=1, source_target_pairs={{4,0},{8,4},{12,8},{0,12},{5,1},{9,5},{13,9},{1,13},{6,2},{10,6},{... | collective-permute-start | bytes 24968 | tf_op jit(solution)/shard_map/ppermute | solution.py:20
  159.6 6.3 %collective-permute-start.2 = (f32[4,4,20,1]{3,2,1,0:T(8,128)S(1)}, f32[4,4,20,1]{3,2,1,0:T(8,128)S(1)}, u32[]{:S(2)}, u32[]{:S(2)}) collective-permute-start(f32[4,4,20,1]{3,2,1,0:T(8,128)S(1)} %get-tuple-element.23), channel_id=1, source_target_pairs={{0,2},{2,0},{1,3},{3,1},{4,6},{6,4},{5,7},{7,5},{8,10},{10,8},{9,1... | collective-permute-start | bytes 3848 | tf_op jit(solution)/shard_map/ppermute | solution.py:17
  160.5 7.5 %collective-permute-start.3 = (f32[4,4,20,1]{3,2,1,0:T(8,128)S(1)}, f32[4,4,20,1]{3,2,1,0:T(8,128)S(1)}, u32[]{:S(2)}, u32[]{:S(2)}) collective-permute-start(f32[4,4,20,1]{3,2,1,0:T(8,128)S(1)} %get-tuple-element.24), channel_id=1, source_target_pairs={{2,0},{0,2},{3,1},{1,3},{6,4},{4,6},{7,5},{5,7},{10,8},{8,10},{11,... | collective-permute-start | bytes 3848 | tf_op jit(solution)/shard_map/ppermute | solution.py:20
  168.2 1.4 collective-permute-start.4
  168.3 1.4 collective-permute-start.5
  171.2 5.5 %collective-permute-start.6 = (bf16[4,2,2,128]{3,2,1,0:T(2,128)(2,1)S(1)}, bf16[4,2,2,128]{3,2,1,0:T(2,128)(2,1)S(1)}, u32[]{:S(2)}, u32[]{:S(2)}) collective-permute-start(bf16[4,2,2,128]{3,2,1,0:T(2,128)(2,1)S(1)} %get-tuple-element.42), channel_id=1, source_target_pairs={{0,4},{4,8},{8,12},{12,0},{1,5},{5,9},{9,13},{13,1},{2,6},{6,10},{... | collective-permute-start | bytes 12296 | tf_op jit(solution)/shard_map/ppermute | solution.py:17
  171.2 5.4 %collective-permute-start.7 = (bf16[4,2,2,128]{3,2,1,0:T(2,128)(2,1)S(1)}, bf16[4,2,2,128]{3,2,1,0:T(2,128)(2,1)S(1)}, u32[]{:S(2)}, u32[]{:S(2)}) collective-permute-start(bf16[4,2,2,128]{3,2,1,0:T(2,128)(2,1)S(1)} %get-tuple-element.43), channel_id=1, source_target_pairs={{4,0},{8,4},{12,8},{0,12},{5,1},{9,5},{13,9},{1,13},{6,2},{10,6},{... | collective-permute-start | bytes 12296 | tf_op jit(solution)/shard_map/ppermute | solution.py:20
  176.7 4.2 %collective-permute-start.8 = (bf16[4,2,20,2]{3,2,1,0:T(8,128)(2,1)S(1)}, bf16[4,2,20,2]{3,2,1,0:T(8,128)(2,1)S(1)}, u32[]{:S(2)}, u32[]{:S(2)}) collective-permute-start(bf16[4,2,20,2]{3,2,1,0:T(8,128)(2,1)S(1)} %get-tuple-element.40), channel_id=1, source_target_pairs={{0,2},{2,0},{1,3},{3,1},{4,6},{6,4},{5,7},{7,5},{8,10},{10,8},{9,1... | collective-permute-start | bytes 1928 | tf_op jit(solution)/shard_map/ppermute | solution.py:17
  177.8 4.1 %collective-permute-start.9 = (bf16[4,2,20,2]{3,2,1,0:T(8,128)(2,1)S(1)}, bf16[4,2,20,2]{3,2,1,0:T(8,128)(2,1)S(1)}, u32[]{:S(2)}, u32[]{:S(2)}) collective-permute-start(bf16[4,2,20,2]{3,2,1,0:T(8,128)(2,1)S(1)} %get-tuple-element.41), channel_id=1, source_target_pairs={{2,0},{0,2},{3,1},{1,3},{6,4},{4,6},{7,5},{5,7},{10,8},{8,10},{11,... | collective-permute-start | bytes 1928 | tf_op jit(solution)/shard_map/ppermute | solution.py:20
  182.0 1.4 collective-permute-start.10
  182.1 1.4 collective-permute-start.11
  183.6 4.4 %copy-start.7 = (bf16[16,4,3,3,3]{0,1,4,3,2:T(4,128)(2,1)S(1)}, bf16[16,4,3,3,3]{0,1,4,3,2:T(4,128)(2,1)}, u32[]{:S(2)}) copy-start(bf16[16,4,3,3,3]{0,1,4,3,2:T(4,128)(2,1)} %param.15) | copy-start | bytes 10372
  183.6 4.4 %copy-start.8 = (f32[16]{0:T(128)S(1)}, f32[16]{0:T(128)}, u32[]{:S(2)}) copy-start(f32[16]{0:T(128)} %param.16) | copy-start | bytes 196
  183.6 4.4 %copy-start.9 = (pred[8,17]{0,1:T(8,128)(4,1)S(1)}, pred[8,17]{0,1:T(8,128)(4,1)}, u32[]{:S(2)}) copy-start(pred[8,17]{0,1:T(8,128)(4,1)} %constant.117) | copy-start | bytes 412
  204.9 3.5 %copy-start.6 = (f32[16]{0:T(128)S(1)}, f32[16]{0:T(128)}, u32[]{:S(2)}) copy-start(f32[16]{0:T(128)} %param.18) | copy-start | bytes 196
  208.6 5.5 %collective-permute-start.12 = (bf16[16,2,1,128]{3,0,2,1:T(8,128)(2,1)S(1)}, bf16[16,2,1,128]{3,0,2,1:T(8,128)(2,1)S(1)}, u32[]{:S(2)}, u32[]{:S(2)}) collective-permute-start(bf16[16,2,1,128]{3,0,2,1:T(8,128)(2,1)S(1)} %get-tuple-element.31), channel_id=1, source_target_pairs={{0,4},{4,8},{8,12},{12,0},{1,5},{5,9},{9,13},{13,1},{2,6},{6,10},{... | collective-permute-start | bytes 24584 | tf_op jit(solution)/shard_map/ppermute | solution.py:17
  209.5 4.6 %collective-permute-start.13 = (bf16[16,2,1,128]{3,0,2,1:T(8,128)(2,1)S(1)}, bf16[16,2,1,128]{3,0,2,1:T(8,128)(2,1)S(1)}, u32[]{:S(2)}, u32[]{:S(2)}) collective-permute-start(bf16[16,2,1,128]{3,0,2,1:T(8,128)(2,1)S(1)} %get-tuple-element.32), channel_id=1, source_target_pairs={{4,0},{8,4},{12,8},{0,12},{5,1},{9,5},{13,9},{1,13},{6,2},{10,6},{... | collective-permute-start | bytes 24584 | tf_op jit(solution)/shard_map/ppermute | solution.py:20
  214.3 6.8 %collective-permute-start.14 = (bf16[16,2,18,1]{3,0,2,1:T(8,128)(2,1)S(1)}, bf16[16,2,18,1]{3,0,2,1:T(8,128)(2,1)S(1)}, u32[]{:S(2)}, u32[]{:S(2)}) collective-permute-start(bf16[16,2,18,1]{3,0,2,1:T(8,128)(2,1)S(1)} %get-tuple-element.29), channel_id=1, source_target_pairs={{0,2},{2,0},{1,3},{3,1},{4,6},{6,4},{5,7},{7,5},{8,10},{10,8},{9,1... | collective-permute-start | bytes 3464 | tf_op jit(solution)/shard_map/ppermute | solution.py:17
  215.5 7.3 %collective-permute-start.15 = (bf16[16,2,18,1]{3,0,2,1:T(8,128)(2,1)S(1)}, bf16[16,2,18,1]{3,0,2,1:T(8,128)(2,1)S(1)}, u32[]{:S(2)}, u32[]{:S(2)}) collective-permute-start(bf16[16,2,18,1]{3,0,2,1:T(8,128)(2,1)S(1)} %get-tuple-element.30), channel_id=1, source_target_pairs={{2,0},{0,2},{3,1},{1,3},{6,4},{4,6},{7,5},{5,7},{10,8},{8,10},{11,... | collective-permute-start | bytes 3464 | tf_op jit(solution)/shard_map/ppermute | solution.py:20
  223.0 1.4 collective-permute-start.16
  223.1 1.6 collective-permute-start.17
  298.2 16.3 %copy-start.5 = (bf16[3,16]{1,0:T(4,128)(2,1)S(1)}, bf16[3,16]{1,0:T(4,128)(2,1)}, u32[]{:S(2)}) copy-start(bf16[3,16]{1,0:T(4,128)(2,1)} %param.19) | copy-start | bytes 292
where the time goes:
time: 316 us
  other arithmetic  127 us (40%)
  local copies, waits for them, and re-layouts  95.1 us (30%)
  starting transfers between devices  31.4 us (10%)
  waiting for transfers between devices  30.5 us (10%)
  matrix products  17.8 us (6%)
  blocking collectives  12.9 us (4%)
    scatter-add x1, other arithmetic, on_device(): painted = jnp.zeros((paint_values.shape[0], extent_cells), jnp.float32).a...  101 us
    gather x1, local copies, waits for them, and re-layouts, sample(): jnp.take(widened.reshape(channels, -1), flat_index.reshape(-1), axis=1)  57.5 us
    ppermute x9, waiting for transfers between devices, padded(): lax.ppermute(lax.slice_in_dim(block, block.shape[dim] - width, None, axis...  17.5 us
    conv_general_dilated x2, matrix products, convolve(): lax.conv_general_dilated(widened[None], weight, (1, 1, 1), 'VALID', dimen...  16.8 us
    ppermute x9, starting transfers between devices, padded(): lax.ppermute(lax.slice_in_dim(block, 0, width, axis=dim), axis, backward)  14.5 us
    all_to_all x1, blocking collectives, on_device(): lax.all_to_all(sampled, ('gx', 'gy'), split_axis=1, concat_axis=1, tiled=...  12.9 us
    conv_general_dilated x5, local copies, waits for them, and re-layouts, convolve(): lax.conv_general_dilated(widened[None], weight, (1, 1, 1), 'VALID', dimen...  7.75 us
    all_to_all x1, starting transfers between devices, on_device(): lax.all_to_all(send_rows, ('gx', 'gy'), split_axis=1, concat_axis=1, tile...  7.3 us
  transfers between devices with their start and end apart: 20, of which 17 were waited for; matrix products, arithmetic and copies ran while one was open for 2% of the time, Pallas kernels for 0%

commit v1 on v0

v1 whole, which is shorter than its diff:
```python
import functools
import jax
import jax.numpy as jnp
from jax import lax
from jax.experimental import pallas as pl
from jax.experimental.pallas import tpu as pltpu
from jax.sharding import PartitionSpec as P

TX = 16
TY = 128
TZ = 2
SEGMENT = 256
F32 = jnp.float32
BF16 = jnp.bfloat16
VMEM_SPEC = pl.BlockSpec(memory_space=pltpu.VMEM)
SMEM_SPEC = pl.BlockSpec(memory_space=pltpu.SMEM)


def exchange_pairs(count, step):
    if count & (count - 1) == 0:
        return [(i, i ^ step) for i in range(count)]
    return [(i, (i + step) % count) for i in range(count)]


def return_pairs(count, step):
    return [(target, source) for source, target in exchange_pairs(count, step)]


def rows_iota(rows, lanes):
    return lax.broadcasted_iota(jnp.int32, (rows, lanes), 0).astype(F32)


def hat(distance):
    return jnp.maximum(1.0 - jnp.abs(distance), 0.0)


def wrapped_x(px, x_start, nx):
    rel = px - x_start
    rel = jnp.where(rel < -1.0, rel + nx, rel)
    return jnp.where(rel > nx - 1.0, rel - nx, rel)


def write_y_weights(py, ny, high_ref, low_ref):
    lanes = py.shape[1]
    base = jnp.floor(py + 0.5)
    frac = py - base
    near = base + jnp.where(frac >= 0.0, 1.0, -1.0)
    base = jnp.where(base >= ny, base - ny, base)
    near = jnp.where(near < 0.0, near + ny, near)
    near = jnp.where(near >= ny, near - ny, near)
    w_near = jnp.abs(frac)
    w_base = 1.0 - w_near

    def tiled(row):
        return jnp.broadcast_to(row, (16, lanes)).astype(BF16)

    bh, nh = tiled(w_base), tiled(w_near)
    if low_ref is not None:
        bl = (jnp.broadcast_to(w_base, (16, lanes)) - bh.astype(F32)).astype(BF16)
        nl = (jnp.broadcast_to(w_near, (16, lanes)) - nh.astype(F32)).astype(BF16)
    index = lax.broadcasted_iota(jnp.int32, (16, lanes), 0).astype(F32).astype(BF16)
    zero = jnp.zeros((16, lanes), BF16)
    for start in range(0, ny, SEGMENT):
        length = min(SEGMENT, ny - start)
        at_base = tiled(jnp.clip(base - start, -1.0, SEGMENT))
        at_near = tiled(jnp.clip(near - start, -1.0, SEGMENT))
        for row in range(0, length, 16):
            here = index + jnp.asarray(row, BF16)
            on_base, on_near = here == at_base, here == at_near
            rows = pl.ds(start + row, 16)
            high_ref[rows, :] = jnp.where(on_base, bh, jnp.where(on_near, nh, zero))
            if low_ref is not None:
                low_ref[rows, :] = jnp.where(on_base, bl, jnp.where(on_near, nl, zero))


def paint_kernel(nz, nx, ny, counts, first, *refs):
    place = refs[0]
    sources = refs[1 : 1 + len(counts)]
    refs = refs[1 + len(counts) :]
    if not first:
        before, refs = refs[0], refs[1:]
    outs, (rows_ref, a_ref, wh_ref, wl_ref, acc) = refs[:-5], refs[-5:]
    ext = TX + 4
    per_x = nz * 4
    half = ext * per_x
    total = 0
    for source, count in zip(sources, counts):
        for index in range(count):
            rows_ref[total] = source[pl.ds(8 * index, 8), :]
            total += 1
    x_start = place[0]
    if first:
        acc[...] = jnp.zeros_like(acc)
    else:
        acc[...] = before[...]

    def one_block(index, carry):
        rows = rows_ref[index]
        lanes = rows.shape[1]
        write_y_weights(rows[2:3], ny, wh_ref, wl_ref)
        rel = wrapped_x(rows[1:2], x_start, nx)
        wx = hat(rows_iota(24, lanes) - rel)
        plane = lax.broadcasted_iota(jnp.int32, (per_x, lanes), 0)
        wz = hat((plane // 4).astype(F32) - rows[0:1])
        channel = plane % 4
        value = jnp.where(
            channel == 0,
            rows[3:4],
            jnp.where(channel == 1, rows[4:5], jnp.where(channel == 2, rows[5:6], rows[6:7])),
        )
        spread = wz * value
        for x in range(ext):
            full = spread * wx[x : x + 1]
            high = full.astype(BF16)
            a_ref[pl.ds(x * per_x, per_x), :] = high
            a_ref[pl.ds(half + x * per_x, per_x), :] = (full - high.astype(F32)).astype(BF16)
        dims = (((1,), (1,)), ((), ()))
        main = lax.dot_general(a_ref[...], wh_ref[...], dims, preferred_element_type=F32)
        side = lax.dot_general(
            a_ref[pl.ds(0, half), :], wl_ref[...], dims, preferred_element_type=F32
        )
        acc[...] += main[:half] + main[half:] + side
        return carry

    lax.fori_loop(0, total, one_block, 0)
    if len(outs) == 1:
        outs[0][...] = acc[...]
    else:
        keep, send = outs
        width = keep.shape[0]
        sub = TX * per_x // 2
        level = place[1].astype(jnp.int32)
        keep[...] = acc[pl.ds(pl.multiple_of(level * sub, sub), width), :]
        send[...] = acc[pl.ds(pl.multiple_of((1 - level) * sub, sub), width), :]


def paint(place, sources, before, nz, nx, ny, split):
    counts = [source.shape[0] // 8 for source in sources]
    lanes = sources[0].shape[1]
    per_x = nz * 4
    half = (TX + 4) * per_x
    if split:
        shape = jax.ShapeDtypeStruct(((TX // 2 + 4) * per_x, ny), F32)
        out_shape = (shape, shape)
        out_specs = (VMEM_SPEC, VMEM_SPEC)
    else:
        out_shape = jax.ShapeDtypeStruct((half, ny), F32)
        out_specs = VMEM_SPEC
    args = [place] + list(sources) + ([] if before is None else [before])
    return pl.pallas_call(
        functools.partial(paint_kernel, nz, nx, ny, counts, before is None),
        out_shape=out_shape,
        in_specs=[SMEM_SPEC] + [VMEM_SPEC] * (len(args) - 1),
        out_specs=out_specs,
        scratch_shapes=[
            pltpu.VMEM((sum(counts), 8, lanes), F32),
            pltpu.VMEM((2 * half, lanes), BF16),
            pltpu.VMEM((ny, lanes), BF16),
            pltpu.VMEM((ny, lanes), BF16),
            pltpu.VMEM((half, ny), F32),
        ],
        cost_estimate=pl.CostEstimate(
            flops=6 * half * lanes * ny * sum(counts),
            bytes_accessed=4 * half * ny,
            transcendentals=0,
        ),
        name="paint",
    )(*args)


def prepare_kernel(nz, w1_ref, w2_ref, b1_ref, b2_ref, hw_ref, o1, o2, ob1, ob2, oh, t1, t2):
    per_in = nz * 4
    per_mid = nz * 16
    t1[...] = jnp.zeros_like(t1)
    t2[...] = jnp.zeros_like(t2)
    oh[...] = jnp.zeros_like(oh)

    def at(a, b, e):
        return (a * 3 + b) * 3 + e

    for b in range(3):
        for e in range(3):
            for q in range(2):
                xi = q + b
                for zo in range(nz):
                    for a in range(3):
                        zi = zo + a - 1
                        if zi < 0 or zi >= nz:
                            continue
                        t1[
                            pl.ds((e * 4 + xi) * per_in + zi * 4, 4),
                            pl.ds((q * nz + zo) * 16, 16),
                        ] = w1_ref[at(a, b, e)].astype(F32)
                        t2[
                            pl.ds(((e * 2 + q) * nz + zo) * 16, 16),
                            pl.ds((xi * nz + zi) * 16, 16),
                        ] = w2_ref[at(a, b, e)].astype(F32)
    o1[...] = t1[...].T.astype(BF16)
    o2[...] = t2[...].astype(BF16)
    for q in range(2 * nz):
        oh[pl.ds(q * 4, 3), pl.ds(q * 16, 16)] = hw_ref[...].astype(F32)
    for source, target in ((b1_ref, ob1), (b2_ref, ob2)):
        shape = (2 * per_mid, 16)
        pick = lax.broadcasted_iota(jnp.int32, shape, 0) % 16 == lax.broadcasted_iota(
            jnp.int32, shape, 1
        )
        target[...] = jnp.sum(
            jnp.where(pick, jnp.broadcast_to(source[...], shape), 0.0), axis=1, keepdims=True
        )


def prepare(conv1_weight, conv1_bias, conv2_weight, conv2_bias, head_weight, nz):
    w1 = jnp.transpose(conv1_weight, (2, 3, 4, 1, 0)).reshape(27, 4, 16)
    w2 = jnp.transpose(conv2_weight, (2, 3, 4, 0, 1)).reshape(27, 16, 16)
    rows = 2 * nz * 16
    return pl.pallas_call(
        functools.partial(prepare_kernel, nz),
        out_shape=(
            jax.ShapeDtypeStruct((rows, 3 * 4 * nz * 4), BF16),
            jax.ShapeDtypeStruct((3 * rows, 4 * nz * 16), BF16),
            jax.ShapeDtypeStruct((rows, 1), F32),
            jax.ShapeDtypeStruct((rows, 1), F32),
            jax.ShapeDtypeStruct((2 * nz * 4, rows), F32),
        ),
        in_specs=[VMEM_SPEC] * 5,
        out_specs=(VMEM_SPEC,) * 5,
        scratch_shapes=[
            pltpu.VMEM((3 * 4 * nz * 4, rows), F32),
            pltpu.VMEM((3 * rows, 4 * nz * 16), F32),
        ],
        cost_estimate=pl.CostEstimate(flops=1000000, bytes_accessed=1000000, transcendentals=0),
        name="prepare",
    )(w1, w2, conv1_bias[None], conv2_bias[None], head_weight)


def silu(v):
    return v / (1.0 + jnp.exp(-v))


def mesh_kernel(nz, keep, got, w1, w2, b1, b2, hw, out, d3, hid):
    per_in = nz * 4
    per_mid = nz * 16
    ny = keep.shape[1]
    width = keep.shape[0] // per_in
    density = (keep[...] + got[...]).astype(BF16)
    wide = density.astype(F32)
    d3[0] = pltpu.roll(wide, 1, 1).astype(BF16)
    d3[1] = density
    d3[2] = pltpu.roll(wide, ny - 1, 1).astype(BF16)
    for x in range(0, width - 2, 2):
        window = pl.ds(x * per_in, 4 * per_in)
        taps = jnp.concatenate([d3[0, window, :], d3[1, window, :], d3[2, window, :]], axis=0)
        summed = jnp.dot(w1[...], taps, preferred_element_type=F32)
        hid[pl.ds(x * per_mid, 2 * per_mid), :] = silu(summed + b1[...]).astype(BF16)
    head = hw[...].astype(BF16)
    rows = 2 * per_mid
    for x in range(0, width - 4, 2):
        parts = jnp.dot(
            w2[...], hid[pl.ds(x * per_mid, 4 * per_mid), :], preferred_element_type=F32
        )
        summed = (
            pltpu.roll(parts[:rows], 1, 1)
            + parts[rows : 2 * rows]
            + pltpu.roll(parts[2 * rows :], ny - 1, 1)
        )
        features = silu(summed + b2[...]).astype(BF16)
        out[pl.ds(x * per_in, 2 * per_in), :] = jnp.dot(
            head, features, preferred_element_type=F32
        )


def mesh_step(keep, got, weights, nz):
    per_in = nz * 4
    ny = keep.shape[1]
    width = keep.shape[0] // per_in
    return pl.pallas_call(
        functools.partial(mesh_kernel, nz),
        out_shape=jax.ShapeDtypeStruct(((width - 4) * per_in, ny), F32),
        in_specs=[VMEM_SPEC] * 7,
        out_specs=VMEM_SPEC,
        scratch_shapes=[
            pltpu.VMEM((3, keep.shape[0], ny), BF16),
            pltpu.VMEM(((width - 2) * nz * 16, ny), BF16),
        ],
        name="mesh_step",
    )(keep, got, *weights)


def sample_kernel(nz, nx, ny, place, own, other, *refs):
    count = (len(refs) - 3) // 2
    sources, outs = refs[:count], refs[count : 2 * count]
    f_ref, wh_ref, t_ref = refs[2 * count :]
    per_x = nz * 4
    span = own.shape[0]
    half = 2 * span
    for index, source in enumerate((own, other)):
        full = source[...]
        high = full.astype(BF16)
        f_ref[pl.ds(index * span, span), :] = high
        f_ref[pl.ds(half + index * span, span), :] = (full - high.astype(F32)).astype(BF16)
    x_start = place[0] + 2.0
    level = place[1]
    width = span // per_x
    for source, out in zip(sources, outs):
        lanes = source.shape[1]
        write_y_weights(source[2:3, :], ny, wh_ref, None)
        t_ref[...] = jnp.dot(f_ref[...], wh_ref[...], preferred_element_type=F32)
        rel = wrapped_x(source[1:2, :], x_start, nx)
        total = jnp.zeros((per_x, lanes), F32)
        for index, offset in enumerate((level * width, (1.0 - level) * width)):
            wx = hat(rows_iota(8 * ((width + 7) // 8), lanes) + (offset - rel))
            for x in range(width):
                row = index * span + x * per_x
                total += wx[x : x + 1] * (
                    t_ref[pl.ds(row, per_x), :] + t_ref[pl.ds(half + row, per_x), :]
                )
        plane = lax.broadcasted_iota(jnp.int32, (per_x, lanes), 0)
        total = total * hat((plane // 4).astype(F32) - source[0:1, :])
        summed = total[0:4]
        for z in range(1, nz):
            summed = summed + total[z * 4 : z * 4 + 4]
        out[...] = summed


def sample(place, own, other, sources, nz, nx, ny):
    lanes = sources[0].shape[1]
    span = own.shape[0]
    return pl.pallas_call(
        functools.partial(sample_kernel, nz, nx, ny),
        out_shape=tuple(jax.ShapeDtypeStruct((4, lanes), F32) for _ in sources),
        in_specs=[SMEM_SPEC] + [VMEM_SPEC] * (2 + len(sources)),
        out_specs=tuple(VMEM_SPEC for _ in sources),
        scratch_shapes=[
            pltpu.VMEM((4 * span, ny), BF16),
            pltpu.VMEM((ny, lanes), BF16),
            pltpu.VMEM((4 * span, lanes), F32),
        ],
        cost_estimate=pl.CostEstimate(
            flops=8 * span * lanes * ny * len(sources),
            bytes_accessed=8 * span * ny,
            transcendentals=0,
        ),
        name="sample",
    )(place, own, other, *sources)


def on_device(
    offsets,
    particle_mass,
    velocity,
    home_cell,
    home_tile,
    conv1_weight,
    conv1_bias,
    conv2_weight,
    conv2_bias,
    head_weight,
):
    columns = lax.axis_size("gy")
    rows = lax.axis_size("gx")
    levels = lax.axis_size("gz")
    assert levels == 2
    nz, nx, ny = TZ * levels, TX * rows, TY * columns
    level = lax.axis_index("gz")
    base_z = home_cell // (TX * TY) + level * TZ
    base_x = home_tile // columns * TX + home_cell // TY % TX
    base_y = home_tile % columns * TY + home_cell % TY
    base = jnp.stack([base_z, base_x, base_y]).astype(F32)
    block = jnp.concatenate(
        [
            base + offsets,
            particle_mass[None],
            particle_mass[None] * velocity,
            jnp.zeros_like(particle_mass)[None],
        ],
        axis=0,
    )
    place = jnp.stack([lax.axis_index("gx") * TX - 2, level]).astype(F32)
    line = jnp.concatenate(
        [block]
        + [lax.ppermute(block, "gy", exchange_pairs(columns, s)) for s in range(1, columns)],
        axis=0,
    )
    arrived = [lax.ppermute(line, "gx", exchange_pairs(rows, s)) for s in range(1, rows)]
    weights = prepare(conv1_weight, conv1_bias, conv2_weight, conv2_bias, head_weight, nz)
    early = paint(place, [line], None, nz, nx, ny, False)
    keep, send = paint(place, arrived, early, nz, nx, ny, True)
    got = lax.ppermute(send, "gz", exchange_pairs(levels, 1))
    own = mesh_step(keep, got, weights, nz)
    other = lax.ppermute(own, "gz", exchange_pairs(levels, 1))
    away = sample(place, own, other, [part[:8] for part in arrived], nz, nx, ny)
    home = [
        lax.ppermute(part, "gx", return_pairs(rows, s)) for s, part in enumerate(away, start=1)
    ]
    (here,) = sample(place, own, other, [block], nz, nx, ny)
    for part in home:
        here = here + part
    return here[:3]


def solution(mesh):
    in_specs = (
        P(None, ("runs", "gx", "gy", "gz")),
        P(("runs", "gx", "gy", "gz")),
        P(None, ("runs", "gx", "gy", "gz")),
        P(("runs", "gx", "gy", "gz")),
        P(("runs", "gx", "gy", "gz")),
        P(),
        P(),
        P(),
        P(),
        P(),
    )
    out_specs = P(None, ("runs", "gx", "gy", "gz"))
    return jax.shard_map(
        on_device, mesh=mesh, in_specs=in_specs, out_specs=out_specs, check_vma=False
    )
```

time: 316 us -> 45.8 us (0.14)
  other arithmetic: 127 us -> 2.77 us
  local copies, waits for them, and re-layouts: 95.1 us -> 5.16 us
  waiting for transfers between devices: 30.5 us -> 4.89 us
  Pallas kernels: 0 us -> 19.7 us
  starting transfers between devices: 31.4 us -> 12.8 us
  matrix products: 17.8 us -> 0 us
  blocking collectives: 12.9 us -> 0 us
    scatter-add x1 -> x0, other arithmetic: 101 us -> none  [on_device(): painted = jnp.zeros((paint_values.shape[0], extent_cells), jnp.float32).a...]
    gather x3 -> x0, local copies, waits for them, and re-layouts: 64.8 us -> none  [the longest x1 57.5 us: sample(): jnp.take(widened.reshape(channels, -1), flat_index.reshape(-1), axis=1)]
    pallas_call x0 -> x6, Pallas kernels: none -> 19.7 us  [the longest x2 9.48 us: paint(): pl.pallas_call(functools.partial(paint_kernel, nz, nx, ny, counts, before...]
    ppermute x18 -> x9, waiting for transfers between devices: 22.8 us -> 4.89 us  [the longest x3 2.21 us: on_device(): lax.ppermute(part, 'gx', return_pairs(rows, s))]
    conv_general_dilated x2 -> x0, matrix products: 16.8 us -> none  [convolve(): lax.conv_general_dilated(widened[None], weight, (1, 1, 1), 'VALID', dimen...]
    all_to_all x1 -> x0, blocking collectives: 12.9 us -> none  [on_device(): lax.all_to_all(sampled, ('gx', 'gy'), split_axis=1, concat_axis=1, tiled=...]
    scatter x3 -> x0, local copies, waits for them, and re-layouts: 12.7 us -> none  [the longest x1 5.04 us: on_device(): jnp.zeros((1, tile_count * capacity), jnp.int32).at[:, slot_index]]
    all_to_all x2 -> x0, starting transfers between devices: 11.4 us -> none  [the longest x1 7.3 us: on_device(): lax.all_to_all(send_rows, ('gx', 'gy'), split_axis=1, concat_axis=1, tile...]
  transfers between devices with their start and end apart: 20 -> 9, of which waited for: 17 -> 3; matrix products, arithmetic and copies ran while one was open for 2% -> 6% of each run, Pallas kernels for 0% -> 16%
where the time goes in v1:
time: 45.8 us; the launch traced here: 45.4 us
  Pallas kernels  19.7 us (43%)
  starting transfers between devices  12.8 us (28%)
  local copies, waits for them, and re-layouts  5.16 us (11%)
  waiting for transfers between devices  4.89 us (11%)
  other arithmetic  2.77 us (6%)
    pallas_call x2, Pallas kernels, paint(): pl.pallas_call(functools.partial(paint_kernel, nz, nx, ny, counts, before...  9.48 us
    ppermute x3, starting transfers between devices, on_device(): lax.ppermute(line, 'gx', exchange_pairs(rows, s))  4.84 us
    pallas_call x2, Pallas kernels, sample(): pl.pallas_call(functools.partial(sample_kernel, nz, nx, ny), out_shape=tu...  4.66 us
    ppermute x3, starting transfers between devices, on_device(): lax.ppermute(part, 'gx', return_pairs(rows, s))  4.39 us
    pallas_call x1, Pallas kernels, mesh_step(): pl.pallas_call(functools.partial(mesh_kernel, nz), out_shape=jax.ShapeDty...  3.38 us
    unnamed x26, local copies, waits for them, and re-layouts  3.27 us
    ppermute x1, starting transfers between devices, on_device(): lax.ppermute(block, 'gy', exchange_pairs(columns, s))  3.03 us
    ppermute x3, waiting for transfers between devices, on_device(): lax.ppermute(part, 'gx', return_pairs(rows, s))  2.21 us
  transfers between devices with their start and end apart: 9, of which 3 were waited for; matrix products, arithmetic and copies ran while one was open for 6% of the time, Pallas kernels for 16%

profile of v1, /device:TPU:0, one launch (start us, length us, event | category | flops | bytes accessed | tf_op | source)
XLA Modules:
  0.0 45.4 jit_solution(3123018642187703897)
XLA Ops:
  0.0 0.0 copy-start.5
  0.0 0.0 copy-start.4
  0.0 0.7 %fusion.4 = (s32[1024]{0:T(1024)S(1)}, s32[1024]{0:T(1024)S(1)}, s32[1024]{0:T(1024)S(1)}) fusion(s32[1024]{0:T(1024)} %param.14, s32[1024]{0:T(1024)} %param.13, s32[]{:T(128)S(6)} %mul.25), kind=kLoop, calls=%fused_computation.26 | loop fusion | flops 65536 | bytes 20484 | tf_op jit(solution)/shard_map/add | solution.py:366
  0.7 0.0 copy-start.2
  0.8 0.0 copy-done.5
  0.8 0.0 copy-done.4
  0.8 0.7 %copy-done.2 = f32[1024]{0:T(1024)S(1)} copy-done((f32[1024]{0:T(1024)S(1)}, f32[1024]{0:T(1024)}, u32[]{:S(2)}) %copy-start.2) | copy-done | bytes 4120
  1.5 0.0 copy-start.3
  1.5 3.0 %collective-permute-start = (f32[8,1024]{1,0:T(8,128)S(1)}, f32[8,1024]{1,0:T(8,128)S(1)}, u32[]{:S(2)}, u32[]{:S(2)}) collective-permute-start(f32[8,1024]{1,0:T(8,128)S(1)} %pad_maximum_fusion.refs_0_), channel_id=1, source_target_pairs={{0,2},{2,0},{1,3},{3,1},{4,6},{6,4},{5,7},{7,5},{8,10},{10,8},{9,1... | collective-permute-start | bytes 98312 | tf_op jit(solution)/shard_map/ppermute | solution.py:381
  4.5 0.7 %add_convert_fusion.1.refs_0_.place = f32[2]{0:T(128)} fusion(s32[1]{0:T(128)} %bitcast.1, s32[1]{0:T(128)} %bitcast), kind=kLoop, calls=%fused_computation.36 | loop fusion | flops 4 | bytes 16 | tf_op jit(solution)/shard_map/convert_element_type | solution.py:378
  5.2 1.2 %collective-permute-done = f32[8,1024]{1,0:T(8,128)S(1)} collective-permute-done((f32[8,1024]{1,0:T(8,128)S(1)}, f32[8,1024]{1,0:T(8,128)S(1)}, u32[]{:S(2)}, u32[]{:S(2)}) %collective-permute-start) | collective-permute-done | bytes 32800 | tf_op jit(solution)/shard_map/ppermute | solution.py:381
  6.5 0.0 copy-done.3
  6.5 0.0 copy-start.1
  6.5 4.2 %collective-permute-start.3 = (f32[16,1024]{1,0:T(8,128)S(1)}, f32[16,1024]{1,0:T(8,128)S(1)}, u32[]{:S(2)}, u32[]{:S(2)}) collective-permute-start(f32[16,1024]{1,0:T(8,128)S(1)} %concatenate.8.refs_1_), channel_id=1, source_target_pairs={{0,12},{4,8},{8,4},{12,0},{1,13},{5,9},{9,5},{13,1},{2,14},{6,10},... | collective-permute-start | bytes 196616 | tf_op jit(solution)/shard_map/ppermute | solution.py:384
  10.7 0.0 collective-permute-start.2
  10.7 0.6 %collective-permute-start.1 = (f32[16,1024]{1,0:T(8,128)S(1)}, f32[16,1024]{1,0:T(8,128)S(1)}, u32[]{:S(2)}, u32[]{:S(2)}) collective-permute-start(f32[16,1024]{1,0:T(8,128)S(1)} %concatenate.8.refs_1_), channel_id=1, source_target_pairs={{0,4},{4,0},{8,12},{12,8},{1,5},{5,1},{9,13},{13,9},{2,6},{6,2},{1... | collective-permute-start | bytes 196616 | tf_op jit(solution)/shard_map/ppermute | solution.py:384
  11.3 0.0 copy-done.1
  11.3 3.1 %paint.2.refs_4_ = f32[320,256]{1,0:T(8,128)} custom-call(f32[2]{0:T(128)} %add_convert_fusion.1.refs_0_.place, f32[16,1024]{1,0:T(8,128)} %copy-done.1), custom_call_target="tpu_custom_call" | custom-call | flops 1006632960 | bytes 327680 | tf_op jit(solution)/shard_map/paint/pallas_call | solution.py:150
  14.4 0.0 collective-permute-done.3.refs_3_
  14.4 0.0 copy-start.6
  14.4 1.4 %collective-permute-done.2.refs_2_ = f32[16,1024]{1,0:T(8,128)S(1)} collective-permute-done((f32[16,1024]{1,0:T(8,128)S(1)}, f32[16,1024]{1,0:T(8,128)S(1)}, u32[]{:S(2)}, u32[]{:S(2)}) %collective-permute-start.2) | collective-permute-done | bytes 65568 | tf_op jit(solution)/shard_map/ppermute | solution.py:384
  15.9 0.0 copy-start.8
  15.9 0.0 collective-permute-done.1.refs_1_
  15.9 0.0 copy-done.6
  15.9 0.6 %copy-done.8 = f32[16,1024]{1,0:T(8,128)} copy-done((f32[16,1024]{1,0:T(8,128)}, f32[16,1024]{1,0:T(8,128)S(1)}, u32[]{:S(2)}) %copy-start.8) | copy-done | bytes 65560
  16.5 0.0 copy-start.10
  16.5 0.6 %copy-done.10 = f32[16,1024]{1,0:T(8,128)} copy-done((f32[16,1024]{1,0:T(8,128)}, f32[16,1024]{1,0:T(8,128)S(1)}, u32[]{:S(2)}) %copy-start.10) | copy-done | bytes 65560
  17.1 6.4 %paint.3 = (f32[192,256]{1,0:T(8,128)}, f32[192,256]{1,0:T(8,128)}) custom-call(f32[2]{0:T(128)} %add_convert_fusion.1.refs_0_.place, f32[16,1024]{1,0:T(8,128)} %copy-done.10, f32[16,1024]{1,0:T(8,128)} %copy-done.8, f32[16,1024]{1,0:T(8,128)} %copy-done.6, f32[320,256]{1,0:T(8,128)} %paint.2.refs_4_), custom_call_target="tpu_custom_call" | custom-call | flops 3019898880 | bytes 327680 | tf_op jit(solution)/shard_map/paint/pallas_call | solution.py:150
  23.5 0.0 collective-permute-start.4
  23.5 2.2 %prepare.1 = (bf16[128,192]{1,0:T(8,128)(2,1)}, bf16[384,256]{1,0:T(8,128)(2,1)}, f32[128,1]{1,0:T(8,128)}, f32[128,1]{1,0:T(8,128)}, f32[32,128]{1,0:T(8,128)}) custom-call(bf16[27,4,16]{2,1,0:T(4,128)(2,1)} %bitcast.17, bf16[27,16,16]{2,1,0:T(8,128)(2,1)} %bitcast.14, f32[1,16]{1,0:T(1,128)} %bitcast.21, f32[1,16]{1,0:T(1,128)} %bitcast.22, ...), custom_call_target="tpu_custom_call" | custom-call | flops 1000000 | bytes 1000000 | tf_op jit(solution)/shard_map/prepare/pallas_call | solution.py:216
  25.7 0.0 collective-permute-done.4.got
  25.7 0.0 copy-start
  25.7 0.7 %copy-done = f32[192,256]{1,0:T(8,128)} copy-done((f32[192,256]{1,0:T(8,128)}, f32[192,256]{1,0:T(8,128)S(1)}, u32[]{:S(2)}) %copy-start) | copy-done | bytes 196632
  26.4 0.0 copy-start.7
  26.4 3.4 %mesh_step.1.own = f32[128,256]{1,0:T(8,128)} custom-call(f32[192,256]{1,0:T(8,128)} %get-tuple-element.15.keep, f32[192,256]{1,0:T(8,128)} %copy-done, bf16[128,192]{1,0:T(8,128)(2,1)} %get-tuple-element.17.w1, bf16[384,256]{1,0:T(8,128)(2,1)} %get-tuple-element.18.w2, f32[128,1]{1,0:T(8,128)} %get-tuple-element.19.b1, f32[128,1]{1,0:T(8,128)} %get-tuple-element.20.b2, ...), custom_call_target="tpu_custom_call" | custom-call | tf_op jit(solution)/shard_map/mesh_step/pallas_call | solution.py:276
  29.8 0.0 copy-start.9
  29.8 0.0 copy-start.11
  29.8 0.5 %collective-permute-start.5 = (f32[128,256]{1,0:T(8,128)}, f32[128,256]{1,0:T(8,128)S(1)}, u32[]{:S(2)}, u32[]{:S(2)}) collective-permute-start(f32[128,256]{1,0:T(8,128)} %mesh_step.1.own), channel_id=1, source_target_pairs={{0,1},{1,0},{2,3},{3,2},{4,5},{5,4},{6,7},{7,6},{8,9},{9,8},{10,11... | collective-permute-start | bytes 393224 | tf_op jit(solution)/shard_map/ppermute | solution.py:390
  30.3 0.0 copy-done.7
  30.3 0.6 %slice.18.refs_2_ = f32[8,1024]{1,0:T(8,128)} slice(f32[16,1024]{1,0:T(8,128)S(1)} %copy-done.7), slice={[0:8], [0:1024]} | slice | bytes 65536 | tf_op jit(solution)/shard_map/slice | solution.py:391
  30.9 0.0 copy-done.9
  30.9 0.6 %slice.17.refs_1_ = f32[8,1024]{1,0:T(8,128)} slice(f32[16,1024]{1,0:T(8,128)S(1)} %copy-done.9), slice={[0:8], [0:1024]} | slice | bytes 65536 | tf_op jit(solution)/shard_map/slice | solution.py:391
  31.5 0.0 copy-done.11
  31.5 0.6 %slice.16.refs_0_ = f32[8,1024]{1,0:T(8,128)} slice(f32[16,1024]{1,0:T(8,128)S(1)} %copy-done.11), slice={[0:8], [0:1024]} | slice | bytes 65536 | tf_op jit(solution)/shard_map/slice | solution.py:391
  32.1 0.0 collective-permute-done.5.other
  32.1 0.0 copy-start.12
  32.1 0.7 %copy-done.12 = f32[128,256]{1,0:T(8,128)} copy-done((f32[128,256]{1,0:T(8,128)}, f32[128,256]{1,0:T(8,128)S(1)}, u32[]{:S(2)}) %copy-start.12) | copy-done | bytes 131096
  32.8 2.6 %sample.3 = (f32[4,1024]{1,0:T(4,128)}, f32[4,1024]{1,0:T(4,128)}, f32[4,1024]{1,0:T(4,128)}) custom-call(f32[2]{0:T(128)} %add_convert_fusion.1.refs_0_.place, f32[128,256]{1,0:T(8,128)} %mesh_step.1.own, f32[128,256]{1,0:T(8,128)} %copy-done.12, f32[8,1024]{1,0:T(8,128)} %slice.16.refs_0_, f32[8,1024]{1,0:T(8,128)} %slice.17.refs_1_, f32[8,1024]{1,0:T(8,128)} %slice.18.refs_2_), custom_call_target="tpu_custom_call" | custom-call | flops 805306368 | bytes 262144 | tf_op jit(solution)/shard_map/sample/pallas_call | solution.py:328
  35.4 0.0 collective-permute-start.6
  35.4 2.9 %collective-permute-start.7 = (f32[4,1024]{1,0:T(4,128)}, f32[4,1024]{1,0:T(4,128)S(1)}, u32[]{:S(2)}, u32[]{:S(2)}) collective-permute-start(f32[4,1024]{1,0:T(4,128)} %get-tuple-element.23), channel_id=1, source_target_pairs={{8,0},{12,4},{0,8},{4,12},{9,1},{13,5},{1,9},{5,13},{10,2},{14,6},... | collective-permute-start | bytes 49160 | tf_op jit(solution)/shard_map/ppermute | solution.py:393
  38.3 1.5 %collective-permute-start.8 = (f32[4,1024]{1,0:T(4,128)}, f32[4,1024]{1,0:T(4,128)S(1)}, u32[]{:S(2)}, u32[]{:S(2)}) collective-permute-start(f32[4,1024]{1,0:T(4,128)} %get-tuple-element.24), channel_id=1, source_target_pairs={{12,0},{8,4},{4,8},{0,12},{13,1},{9,5},{5,9},{1,13},{14,2},{10,6},... | collective-permute-start | bytes 49160 | tf_op jit(solution)/shard_map/ppermute | solution.py:393
  39.8 2.0 %sample.2 = f32[4,1024]{1,0:T(4,128)} custom-call(f32[2]{0:T(128)} %add_convert_fusion.1.refs_0_.place, f32[128,256]{1,0:T(8,128)} %mesh_step.1.own, f32[128,256]{1,0:T(8,128)} %copy-done.12, f32[8,1024]{1,0:T(8,128)} %copy-done.3), custom_call_target="tpu_custom_call" | custom-call | flops 268435456 | bytes 262144 | tf_op jit(solution)/shard_map/sample/pallas_call | solution.py:328
  41.8 0.0 collective-permute-done.6
  41.8 0.0 collective-permute-done.7
  41.8 2.2 %collective-permute-done.8 = f32[4,1024]{1,0:T(4,128)S(1)} collective-permute-done((f32[4,1024]{1,0:T(4,128)}, f32[4,1024]{1,0:T(4,128)S(1)}, u32[]{:S(2)}, u32[]{:S(2)}) %collective-permute-start.8) | collective-permute-done | bytes 16416 | tf_op jit(solution)/shard_map/ppermute | solution.py:393
  44.0 1.3 %slice_add_fusion = f32[3,1024]{1,0:T(4,128)} fusion(f32[4,1024]{1,0:T(4,128)S(1)} %collective-permute-done.8, f32[4,1024]{1,0:T(4,128)S(1)} %collective-permute-done.7, f32[4,1024]{1,0:T(4,128)S(1)} %collective-permute-done.6, f32[4,1024]{1,0:T(4,128)} %sample.2), kind=kLoop, calls=%fused_computation.1 | loop fusion | flops 9216 | bytes 61440 | tf_op jit(solution)/shard_map/add | solution.py:397
  (4 shorter events, 0.1 us)
Async XLA Ops:
  0.0 0.8 %copy-start.5 = (f32[3,1024]{1,0:T(4,128)S(1)}, f32[3,1024]{1,0:T(4,128)}, u32[]{:S(2)}) copy-start(f32[3,1024]{1,0:T(4,128)} %param.12) | copy-start | bytes 36868
  0.0 0.8 %copy-start.4 = (f32[3,1024]{1,0:T(4,128)S(1)}, f32[3,1024]{1,0:T(4,128)}, u32[]{:S(2)}) copy-start(f32[3,1024]{1,0:T(4,128)} %param.10) | copy-start | bytes 36868
  0.7 0.7 %copy-start.2 = (f32[1024]{0:T(1024)S(1)}, f32[1024]{0:T(1024)}, u32[]{:S(2)}) copy-start(f32[1024]{0:T(1024)} %param.11) | copy-start | bytes 12292
  1.5 5.0 %copy-start.3 = (f32[8,1024]{1,0:T(8,128)}, f32[8,1024]{1,0:T(8,128)S(1)}, u32[]{:S(2)}) copy-start(f32[8,1024]{1,0:T(8,128)S(1)} %pad_maximum_fusion.refs_0_) | copy-start | bytes 98308
  1.5 4.9 %collective-permute-start = (f32[8,1024]{1,0:T(8,128)S(1)}, f32[8,1024]{1,0:T(8,128)S(1)}, u32[]{:S(2)}, u32[]{:S(2)}) collective-permute-start(f32[8,1024]{1,0:T(8,128)S(1)} %pad_maximum_fusion.refs_0_), channel_id=1, source_target_pairs={{0,2},{2,0},{1,3},{3,1},{4,6},{6,4},{5,7},{7,5},{8,10},{10,8},{9,1... | collective-permute-start | bytes 98312 | tf_op jit(solution)/shard_map/ppermute | solution.py:381
  6.5 4.9 %copy-start.1 = (f32[16,1024]{1,0:T(8,128)}, f32[16,1024]{1,0:T(8,128)S(1)}, u32[]{:S(2)}) copy-start(f32[16,1024]{1,0:T(8,128)S(1)} %concatenate.8.refs_1_) | copy-start | bytes 196612
  6.5 7.9 %collective-permute-start.3 = (f32[16,1024]{1,0:T(8,128)S(1)}, f32[16,1024]{1,0:T(8,128)S(1)}, u32[]{:S(2)}, u32[]{:S(2)}) collective-permute-start(f32[16,1024]{1,0:T(8,128)S(1)} %concatenate.8.refs_1_), channel_id=1, source_target_pairs={{0,12},{4,8},{8,4},{12,0},{1,13},{5,9},{9,5},{13,1},{2,14},{6,10},... | collective-permute-start | bytes 196616 | tf_op jit(solution)/shard_map/ppermute | solution.py:384
  10.7 5.2 %collective-permute-start.2 = (f32[16,1024]{1,0:T(8,128)S(1)}, f32[16,1024]{1,0:T(8,128)S(1)}, u32[]{:S(2)}, u32[]{:S(2)}) collective-permute-start(f32[16,1024]{1,0:T(8,128)S(1)} %concatenate.8.refs_1_), channel_id=1, source_target_pairs={{0,8},{4,12},{8,0},{12,4},{1,9},{5,13},{9,1},{13,5},{2,10},{6,14},... | collective-permute-start | bytes 196616 | tf_op jit(solution)/shard_map/ppermute | solution.py:384
  10.7 5.2 %collective-permute-start.1 = (f32[16,1024]{1,0:T(8,128)S(1)}, f32[16,1024]{1,0:T(8,128)S(1)}, u32[]{:S(2)}, u32[]{:S(2)}) collective-permute-start(f32[16,1024]{1,0:T(8,128)S(1)} %concatenate.8.refs_1_), channel_id=1, source_target_pairs={{0,4},{4,0},{8,12},{12,8},{1,5},{5,1},{9,13},{13,9},{2,6},{6,2},{1... | collective-permute-start | bytes 196616 | tf_op jit(solution)/shard_map/ppermute | solution.py:384
  14.4 1.4 %copy-start.6 = (f32[16,1024]{1,0:T(8,128)}, f32[16,1024]{1,0:T(8,128)S(1)}, u32[]{:S(2)}) copy-start(f32[16,1024]{1,0:T(8,128)S(1)} %collective-permute-done.3.refs_3_) | copy-start | bytes 196612
  15.9 0.6 %copy-start.8 = (f32[16,1024]{1,0:T(8,128)}, f32[16,1024]{1,0:T(8,128)S(1)}, u32[]{:S(2)}) copy-start(f32[16,1024]{1,0:T(8,128)S(1)} %collective-permute-done.2.refs_2_) | copy-start | bytes 196612
  16.5 0.6 %copy-start.10 = (f32[16,1024]{1,0:T(8,128)}, f32[16,1024]{1,0:T(8,128)S(1)}, u32[]{:S(2)}) copy-start(f32[16,1024]{1,0:T(8,128)S(1)} %collective-permute-done.1.refs_1_) | copy-start | bytes 196612
  23.5 2.2 %collective-permute-start.4 = (f32[192,256]{1,0:T(8,128)}, f32[192,256]{1,0:T(8,128)S(1)}, u32[]{:S(2)}, u32[]{:S(2)}) collective-permute-start(f32[192,256]{1,0:T(8,128)} %get-tuple-element.16), channel_id=1, source_target_pairs={{0,1},{1,0},{2,3},{3,2},{4,5},{5,4},{6,7},{7,6},{8,9},{9,8},{10,11... | collective-permute-start | bytes 589832 | tf_op jit(solution)/shard_map/ppermute | solution.py:388
  25.7 0.7 %copy-start = (f32[192,256]{1,0:T(8,128)}, f32[192,256]{1,0:T(8,128)S(1)}, u32[]{:S(2)}) copy-start(f32[192,256]{1,0:T(8,128)S(1)} %collective-permute-done.4.got) | copy-start | bytes 589828
  26.4 3.9 %copy-start.7 = (f32[16,1024]{1,0:T(8,128)S(1)}, f32[16,1024]{1,0:T(8,128)}, u32[]{:S(2)}) copy-start(f32[16,1024]{1,0:T(8,128)} %copy-done.6) | copy-start | bytes 196612
  29.8 1.1 %copy-start.9 = (f32[16,1024]{1,0:T(8,128)S(1)}, f32[16,1024]{1,0:T(8,128)}, u32[]{:S(2)}) copy-start(f32[16,1024]{1,0:T(8,128)} %copy-done.8) | copy-start | bytes 196612
  29.8 1.8 %copy-start.11 = (f32[16,1024]{1,0:T(8,128)S(1)}, f32[16,1024]{1,0:T(8,128)}, u32[]{:S(2)}) copy-start(f32[16,1024]{1,0:T(8,128)} %copy-done.10) | copy-start | bytes 196612
  29.8 2.4 %collective-permute-start.5 = (f32[128,256]{1,0:T(8,128)}, f32[128,256]{1,0:T(8,128)S(1)}, u32[]{:S(2)}, u32[]{:S(2)}) collective-permute-start(f32[128,256]{1,0:T(8,128)} %mesh_step.1.own), channel_id=1, source_target_pairs={{0,1},{1,0},{2,3},{3,2},{4,5},{5,4},{6,7},{7,6},{8,9},{9,8},{10,11... | collective-permute-start | bytes 393224 | tf_op jit(solution)/shard_map/ppermute | solution.py:390
  32.1 0.7 %copy-start.12 = (f32[128,256]{1,0:T(8,128)}, f32[128,256]{1,0:T(8,128)S(1)}, u32[]{:S(2)}) copy-start(f32[128,256]{1,0:T(8,128)S(1)} %collective-permute-done.5.other) | copy-start | bytes 393220
  35.4 6.4 %collective-permute-start.6 = (f32[4,1024]{1,0:T(4,128)}, f32[4,1024]{1,0:T(4,128)S(1)}, u32[]{:S(2)}, u32[]{:S(2)}) collective-permute-start(f32[4,1024]{1,0:T(4,128)} %get-tuple-element.22), channel_id=1, source_target_pairs={{4,0},{0,4},{12,8},{8,12},{5,1},{1,5},{13,9},{9,13},{6,2},{2,6},{1... | collective-permute-start | bytes 49160 | tf_op jit(solution)/shard_map/ppermute | solution.py:393
  35.4 6.4 %collective-permute-start.7 = (f32[4,1024]{1,0:T(4,128)}, f32[4,1024]{1,0:T(4,128)S(1)}, u32[]{:S(2)}, u32[]{:S(2)}) collective-permute-start(f32[4,1024]{1,0:T(4,128)} %get-tuple-element.23), channel_id=1, source_target_pairs={{8,0},{12,4},{0,8},{4,12},{9,1},{13,5},{1,9},{5,13},{10,2},{14,6},... | collective-permute-start | bytes 49160 | tf_op jit(solution)/shard_map/ppermute | solution.py:393
  38.3 5.7 %collective-permute-start.8 = (f32[4,1024]{1,0:T(4,128)}, f32[4,1024]{1,0:T(4,128)S(1)}, u32[]{:S(2)}, u32[]{:S(2)}) collective-permute-start(f32[4,1024]{1,0:T(4,128)} %get-tuple-element.24), channel_id=1, source_target_pairs={{12,0},{8,4},{4,8},{0,12},{13,1},{9,5},{5,9},{1,13},{14,2},{10,6},... | collective-permute-start | bytes 49160 | tf_op jit(solution)/shard_map/ppermute | solution.py:393

commit v2 on v1

v2 whole, which is shorter than its diff:
```python
import functools
import jax
import jax.numpy as jnp
from jax import lax
from jax.experimental import pallas as pl
from jax.experimental.pallas import tpu as pltpu
from jax.sharding import PartitionSpec as P

TX = 16
TY = 128
TZ = 2
SEGMENT = 256
F32 = jnp.float32
BF16 = jnp.bfloat16
VMEM_SPEC = pl.BlockSpec(memory_space=pltpu.VMEM)
SMEM_SPEC = pl.BlockSpec(memory_space=pltpu.SMEM)


def exchange_pairs(count, step):
    if count & (count - 1) == 0:
        return [(i, i ^ step) for i in range(count)]
    return [(i, (i + step) % count) for i in range(count)]


def return_pairs(count, step):
    return [(target, source) for source, target in exchange_pairs(count, step)]


def rows_iota(rows, lanes):
    return lax.broadcasted_iota(jnp.int32, (rows, lanes), 0).astype(F32)


def hat(distance):
    return jnp.maximum(1.0 - jnp.abs(distance), 0.0)


def wrapped_x(px, x_start, nx):
    rel = px - x_start
    rel = jnp.where(rel < -1.0, rel + nx, rel)
    return jnp.where(rel > nx - 1.0, rel - nx, rel)


def write_y_weights(py, ny, high_ref, low_ref):
    lanes = py.shape[1]
    base = jnp.floor(py + 0.5)
    frac = py - base
    near = base + jnp.where(frac >= 0.0, 1.0, -1.0)
    base = jnp.where(base >= ny, base - ny, base)
    near = jnp.where(near < 0.0, near + ny, near)
    near = jnp.where(near >= ny, near - ny, near)
    w_near = jnp.abs(frac)
    w_base = 1.0 - w_near

    def tiled(row):
        return jnp.broadcast_to(row, (16, lanes)).astype(BF16)

    bh, nh = tiled(w_base), tiled(w_near)
    if low_ref is not None:
        bl = (jnp.broadcast_to(w_base, (16, lanes)) - bh.astype(F32)).astype(BF16)
        nl = (jnp.broadcast_to(w_near, (16, lanes)) - nh.astype(F32)).astype(BF16)
    index = lax.broadcasted_iota(jnp.int32, (16, lanes), 0).astype(F32).astype(BF16)
    zero = jnp.zeros((16, lanes), BF16)
    for start in range(0, ny, SEGMENT):
        length = min(SEGMENT, ny - start)
        at_base = tiled(jnp.clip(base - start, -1.0, SEGMENT))
        at_near = tiled(jnp.clip(near - start, -1.0, SEGMENT))
        for row in range(0, length, 16):
            here = index + jnp.asarray(row, BF16)
            on_base, on_near = here == at_base, here == at_near
            rows = pl.ds(start + row, 16)
            high_ref[rows, :] = jnp.where(on_base, bh, jnp.where(on_near, nh, zero))
            if low_ref is not None:
                low_ref[rows, :] = jnp.where(on_base, bl, jnp.where(on_near, nl, zero))


def nbytes(shapes):
    total = 0
    for shape in shapes:
        size = jnp.dtype(shape.dtype).itemsize
        for extent in shape.shape:
            size *= extent
        total += size
    return total


def run_kernel(kernel, name, args, out_shape, scratch, flops=0, smem=1):
    outs = out_shape if isinstance(out_shape, tuple) else (out_shape,)
    moved = nbytes(args) + nbytes(outs)
    grant = moved + nbytes(scratch) + (4 << 20)
    specs = [SMEM_SPEC] * smem + [VMEM_SPEC] * (len(args) - smem)
    return pl.pallas_call(
        kernel,
        out_shape=out_shape,
        in_specs=specs,
        out_specs=tuple(VMEM_SPEC for _ in outs) if isinstance(out_shape, tuple) else VMEM_SPEC,
        scratch_shapes=[pltpu.VMEM(shape.shape, shape.dtype) for shape in scratch],
        compiler_params=pltpu.CompilerParams(vmem_limit_bytes=min(grant, 62 << 20)),
        cost_estimate=pl.CostEstimate(flops=flops, bytes_accessed=moved, transcendentals=0),
        name=name,
    )(*args)


def array(shape, dtype):
    return jax.ShapeDtypeStruct(shape, dtype)


def paint_kernel(nx, ny, counts, first, split, *refs):
    place = refs[0]
    sources = refs[1 : 1 + len(counts)]
    refs = refs[1 + len(counts) :]
    if not first:
        before, refs = refs[0], refs[2:]
    outs, (rows_ref, a_ref, wh_ref, wl_ref, acc) = refs[:-5], refs[-5:]
    per_z = (TX + 4) * 4
    half = (TZ + 1) * per_z
    total = 0
    for source, count in zip(sources, counts):
        for index in range(count):
            rows_ref[total] = source[pl.ds(8 * index, 8), :]
            total += 1
    x_start, level = place[0], place[1]
    if first:
        acc[...] = jnp.zeros_like(acc)
    else:
        acc[...] = before[...]

    def one_block(index, carry):
        rows = rows_ref[index]
        lanes = rows.shape[1]
        write_y_weights(rows[2:3], ny, wh_ref, wl_ref)
        rel = wrapped_x(rows[1:2], x_start, nx)
        slot = lax.broadcasted_iota(jnp.int32, (16, lanes), 0)
        column = (slot // 4).astype(F32) - rel
        channel = slot % 4
        value = jnp.where(
            channel == 0,
            rows[3:4],
            jnp.where(channel == 1, rows[4:5], jnp.where(channel == 2, rows[5:6], rows[6:7])),
        )
        spread = [value * hat(rows[0:1] - (level + z)) for z in range(TZ + 1)]
        for x in range(0, TX + 4, 4):
            wx = hat(column + float(x))
            for z in range(TZ + 1):
                full = spread[z] * wx
                high = full.astype(BF16)
                row = z * per_z + x * 4
                a_ref[pl.ds(row, 16), :] = high
                a_ref[pl.ds(half + row, 16), :] = (full - high.astype(F32)).astype(BF16)
        dims = (((1,), (1,)), ((), ()))
        main = lax.dot_general(a_ref[...], wh_ref[...], dims, preferred_element_type=F32)
        side = lax.dot_general(
            a_ref[pl.ds(0, half), :], wl_ref[...], dims, preferred_element_type=F32
        )
        acc[...] += main[:half] + main[half:] + side
        return carry

    lax.fori_loop(0, total, one_block, 0)
    if not split:
        outs[0][...] = acc[...]
        return
    sub = TX // 2 * 4
    width = sub + 16
    own = level.astype(jnp.int32) * sub
    for z in range(TZ + 1):
        rows = pl.ds(z * width, width)
        outs[0][rows, :] = acc[pl.ds(pl.multiple_of(z * per_z + own, 16), width), :]
        outs[1][rows, :] = acc[pl.ds(pl.multiple_of(z * per_z + sub - own, 16), width), :]


def paint(place, sources, before, nx, ny, split):
    counts = [source.shape[0] // 8 for source in sources]
    lanes = sources[0].shape[1]
    half = (TZ + 1) * (TX + 4) * 4
    if split:
        shape = array(((TZ + 1) * (TX // 2 + 4) * 4, ny), F32)
        out_shape = (shape, shape)
    else:
        out_shape = array((half, ny), F32)
    return run_kernel(
        functools.partial(paint_kernel, nx, ny, counts, before is None, split),
        "paint",
        [place] + list(sources) + ([] if before is None else list(before)),
        out_shape,
        [
            array((sum(counts), 8, lanes), F32),
            array((2 * half, lanes), BF16),
            array((ny, lanes), BF16),
            array((ny, lanes), BF16),
            array((half, ny), F32),
        ],
        flops=6 * half * lanes * ny * sum(counts),
    )


def prepare_kernel(nz, w1_ref, w2_ref, b1_ref, b2_ref, hw_ref, o1, o2, ob1, ob2, oh, t1, t2):
    rows = 2 * nz * 16
    width = TX // 2
    t1[...] = jnp.zeros_like(t1)
    t2[...] = jnp.zeros_like(t2)

    def at(a, b, e):
        return (a * 3 + b) * 3 + e

    for b in range(3):
        for e in range(3):
            for zo in range(nz):
                first = max(0, 1 - zo)
                last = min(2, nz - zo)
                zi = zo + first - 1
                taps = [w2_ref[at(a, b, e)].astype(F32) for a in range(first, last + 1)]
                strip = jnp.concatenate(taps, axis=1)
                for q in range(2):
                    t2[
                        pl.ds(((e * 2 + q) * nz + zo) * 16, 16),
                        pl.ds(((q + b) * nz + zi) * 16, strip.shape[1]),
                    ] = strip
                for a in range(first, last + 1):
                    for q in range(2):
                        t1[
                            pl.ds(((e * nz + zo + a - 1) * 4 + q + b) * 4, 4),
                            pl.ds((q * nz + zo) * 16, 16),
                        ] = w1_ref[at(a, b, e)].astype(F32)
    o1[...] = t1[...].T.astype(BF16)
    o2[...] = t2[...].astype(BF16)
    cells = nz * width
    lanes = cells * 16
    repeat = (
        lax.broadcasted_iota(jnp.int32, (16, lanes), 0)
        == lax.broadcasted_iota(jnp.int32, (16, lanes), 1) % 16
    )
    tiled = jnp.dot(
        hw_ref[...], jnp.where(repeat, 1.0, 0.0).astype(BF16), preferred_element_type=F32
    )
    row = lax.broadcasted_iota(jnp.int32, (cells, lanes), 0)
    same = (row % width) * nz + row // width == lax.broadcasted_iota(
        jnp.int32, (cells, lanes), 1
    ) // 16
    for k in range(3):
        oh[pl.ds(k * cells, cells), :] = jnp.where(same, tiled[k : k + 1], 0.0).astype(BF16)
    for source, target in ((b1_ref, ob1), (b2_ref, ob2)):
        shape = (rows, 16)
        pick = lax.broadcasted_iota(jnp.int32, shape, 0) % 16 == lax.broadcasted_iota(
            jnp.int32, shape, 1
        )
        column = jnp.sum(
            jnp.where(pick, jnp.broadcast_to(source[...], shape), 0.0), axis=1, keepdims=True
        )
        target[...] = jnp.broadcast_to(column, target.shape)


def prepare(conv1_weight, conv1_bias, conv2_weight, conv2_bias, head_weight, nz):
    w1 = jnp.transpose(conv1_weight, (2, 3, 4, 1, 0)).reshape(27, 4, 16)
    w2 = jnp.transpose(conv2_weight, (2, 3, 4, 0, 1)).reshape(27, 16, 16)
    rows = 2 * nz * 16
    cells = nz * TX // 2
    return run_kernel(
        functools.partial(prepare_kernel, nz),
        "prepare",
        [w1, w2, conv1_bias[None], conv2_bias[None], head_weight],
        (
            array((rows, 3 * nz * 16), BF16),
            array((3 * rows, 4 * nz * 16), BF16),
            array((rows, 128), F32),
            array((rows, 128), F32),
            array((3 * cells, 16 * cells), BF16),
        ),
        [array((3 * nz * 16, rows), F32), array((3 * rows, 4 * nz * 16), F32)],
        flops=1000000,
        smem=0,
    )


def silu(v):
    return v / (1.0 + jnp.exp(-v))


def mesh_kernel(nz, place, keep, got, w1, w2, b1, b2, hw, out, d3, hid, feat):
    per_mid = nz * 16
    rows = 2 * per_mid
    ny = keep.shape[1]
    span = keep.shape[0] // (TZ + 1)
    width = span // 4
    at_low = place[1] == 0.0
    mine, theirs = keep[...], got[...]
    low = jnp.where(at_low, mine, theirs)
    high = jnp.where(at_low, theirs, mine)
    planes = []
    for z in range(nz):
        part = []
        if z <= TZ:
            part.append(low[z * span : (z + 1) * span])
        if z >= nz - TZ - 1:
            index = z - (nz - TZ - 1)
            part.append(high[index * span : (index + 1) * span])
        planes.append(part[0] if len(part) == 1 else part[0] + part[1])
    wide = jnp.concatenate(planes, axis=0).astype(BF16).astype(F32)
    d3[0] = pltpu.roll(wide, 1, 1)
    d3[1] = wide
    d3[2] = pltpu.roll(wide, ny - 1, 1)

    def spread(bias):
        return jnp.concatenate([bias[...]] * (ny // 128), axis=1)

    def hidden(x):
        taps = [
            d3[e, pl.ds(z * span + x * 4, 16), :].astype(BF16)
            for e in range(3)
            for z in range(nz)
        ]
        summed = jnp.dot(w1[...], jnp.concatenate(taps, axis=0), preferred_element_type=F32)
        hid[pl.ds(x * per_mid, rows), :] = silu(summed + spread(b1)).astype(BF16)

    def features(x):
        parts = jnp.dot(
            w2[...], hid[pl.ds(x * per_mid, 2 * rows), :], preferred_element_type=F32
        )
        summed = (
            pltpu.roll(parts[:rows], 1, 1)
            + parts[rows : 2 * rows]
            + pltpu.roll(parts[2 * rows :], ny - 1, 1)
        )
        feat[pl.ds(x * per_mid, rows), :] = silu(summed + spread(b2)).astype(BF16)

    hidden(0)
    hidden(2)
    for x in range(0, width - 4, 2):
        if x + 4 < width - 2:
            hidden(x + 4)
        features(x)
    out[...] = jnp.dot(hw[...], feat[...], preferred_element_type=F32)


def mesh_step(place, keep, got, weights, nz):
    ny = keep.shape[1]
    width = keep.shape[0] // (TZ + 1) // 4
    return run_kernel(
        functools.partial(mesh_kernel, nz),
        "mesh_step",
        [place, keep, got] + list(weights),
        array((3 * nz * (width - 4), ny), F32),
        [
            array((3, nz * width * 4, ny), F32),
            array(((width - 2) * nz * 16, ny), BF16),
            array(((width - 4) * nz * 16, ny), BF16),
        ],
        flops=200000000,
    )


def sample_kernel(nz, nx, ny, count, *refs):
    place, own, other = refs[:3]
    sources, outs = refs[3 : 3 + count], refs[3 + count : 3 + 2 * count]
    f_ref, wh_ref, t_ref = refs[3 + 2 * count :]
    at_low = place[1] == 0.0
    level = place[1].astype(jnp.int32)
    width = TX // 2
    for k in range(3):
        for z in range(TZ + 1):
            rows = pl.ds(pl.multiple_of((k * nz + level + z) * width, width), width)
            mine, theirs = own[rows, :], other[rows, :]
            both = jnp.concatenate(
                [jnp.where(at_low, mine, theirs), jnp.where(at_low, theirs, mine)], axis=0
            )
            f_ref[pl.ds((k * (TZ + 1) + z) * TX, TX), :] = both.astype(BF16)
    x_start = place[0] + 2.0
    for source, out in zip(sources, outs):
        lanes = source.shape[1]
        write_y_weights(source[2:3, :], ny, wh_ref, None)
        t_ref[...] = jnp.dot(f_ref[...], wh_ref[...], preferred_element_type=F32)
        rel = wrapped_x(source[1:2, :], x_start, nx)
        wx = hat(rows_iota(TX, lanes) - rel)
        both = [wx * hat(source[0:1, :] - (place[1] + z)) for z in range(TZ + 1)]
        for k in range(3):
            total = both[0] * t_ref[pl.ds(k * (TZ + 1) * TX, TX), :]
            for z in range(1, TZ + 1):
                total += both[z] * t_ref[pl.ds((k * (TZ + 1) + z) * TX, TX), :]
            out[pl.ds(k, 1), :] = jnp.sum(total, axis=0, keepdims=True)


def sample(place, own, other, sources, nz, nx, ny):
    lanes = sources[0].shape[1]
    cells = 3 * (TZ + 1) * TX
    return run_kernel(
        functools.partial(sample_kernel, nz, nx, ny, len(sources)),
        "sample",
        [place, own, other] + list(sources),
        tuple(array((3, lanes), F32) for _ in sources),
        [array((cells, ny), BF16), array((ny, lanes), BF16), array((cells, lanes), F32)],
        flops=2 * cells * lanes * ny * len(sources),
    )


def finish_kernel(*refs):
    total = refs[0][...]
    for part in refs[1:-1]:
        total += part[...]
    refs[-1][...] = total


def on_device(
    offsets,
    particle_mass,
    velocity,
    home_cell,
    home_tile,
    conv1_weight,
    conv1_bias,
    conv2_weight,
    conv2_bias,
    head_weight,
):
    columns = lax.axis_size("gy")
    rows = lax.axis_size("gx")
    levels = lax.axis_size("gz")
    assert levels == 2
    nz, nx, ny = TZ * levels, TX * rows, TY * columns
    level = lax.axis_index("gz")
    base_z = home_cell // (TX * TY) + level * TZ
    base_x = home_tile // columns * TX + home_cell // TY % TX
    base_y = home_tile % columns * TY + home_cell % TY
    base = jnp.stack([base_z, base_x, base_y]).astype(F32)
    block = jnp.concatenate(
        [
            base + offsets,
            particle_mass[None],
            particle_mass[None] * velocity,
            jnp.zeros_like(particle_mass)[None],
        ],
        axis=0,
    )
    place = jnp.stack([lax.axis_index("gx") * TX - 2, level]).astype(F32)
    line = jnp.concatenate(
        [block]
        + [lax.ppermute(block, "gy", exchange_pairs(columns, s)) for s in range(1, columns)],
        axis=0,
    )
    arrived = [lax.ppermute(line, "gx", exchange_pairs(rows, s)) for s in range(1, rows)]
    weights = prepare(conv1_weight, conv1_bias, conv2_weight, conv2_bias, head_weight, nz)
    early = paint(place, [line], None, nx, ny, False)
    keep, send = paint(place, arrived, (early, weights[2]), nx, ny, True)
    got = lax.ppermute(send, "gz", exchange_pairs(levels, 1))
    own = mesh_step(place, keep, got, weights, nz)
    other = lax.ppermute(own, "gz", exchange_pairs(levels, 1))
    away = sample(place, own, other, arrived, nz, nx, ny)
    home = [
        lax.ppermute(part, "gx", return_pairs(rows, s)) for s, part in enumerate(away, start=1)
    ]
    (here,) = sample(place, own, other, [block], nz, nx, ny)
    return run_kernel(finish_kernel, "finish", [here] + home, here, [], smem=0)


def solution(mesh):
    in_specs = (
        P(None, ("runs", "gx", "gy", "gz")),
        P(("runs", "gx", "gy", "gz")),
        P(None, ("runs", "gx", "gy", "gz")),
        P(("runs", "gx", "gy", "gz")),
        P(("runs", "gx", "gy", "gz")),
        P(),
        P(),
        P(),
        P(),
        P(),
    )
    out_specs = P(None, ("runs", "gx", "gy", "gz"))
    return jax.shard_map(
        on_device, mesh=mesh, in_specs=in_specs, out_specs=out_specs, check_vma=False
    )
```

time: 45.8 us -> 35.6 us (0.78)
  Pallas kernels: 19.7 us -> 12.5 us
  local copies, waits for them, and re-layouts: 5.16 us -> 0.74 us
  waiting for transfers between devices: 4.89 us -> 8.82 us
  other arithmetic: 2.77 us -> 0.89 us
  starting transfers between devices: 12.8 us -> 12.2 us
    pallas_call x6 -> x7, Pallas kernels: 19.7 us -> 12.5 us  [run_kernel(): pl.pallas_call(kernel, out_shape=out_shape, in_specs=specs, out_specs=tup...]
    unnamed x26 -> x16, local copies, waits for them, and re-layouts: 3.27 us -> 0.7 us
    slice x3 -> x0, local copies, waits for them, and re-layouts: 1.85 us -> none  [on_device(): away = sample(place, own, other, [part[:8] for part in arrived], nz, nx, ny)]
    ppermute x3, waiting for transfers between devices: 1.44 us -> 2.81 us  [on_device(): lax.ppermute(line, 'gx', exchange_pairs(rows, s))]
    ppermute x1, waiting for transfers between devices: 0.01 us -> 1.36 us  [on_device(): got = lax.ppermute(send, 'gz', exchange_pairs(levels, 1))]
    add x1 -> x0, other arithmetic: 1.33 us -> none  [on_device(): here = here + part]
    ppermute x3, waiting for transfers between devices: 2.21 us -> 3.5 us  [on_device(): lax.ppermute(part, 'gx', return_pairs(rows, s))]
    ppermute x1, waiting for transfers between devices: 1.24 us -> 0.01 us  [on_device(): lax.ppermute(block, 'gy', exchange_pairs(columns, s))]
  transfers between devices with their start and end apart: 9 -> 9, of which waited for: 3 -> 6; matrix products, arithmetic and copies ran while one was open for 6% -> 0% of each run, Pallas kernels for 16% -> 14%
where the time goes in v2:
time: 35.6 us; the launch traced here: 35.3 us
  Pallas kernels  12.5 us (35%)
  starting transfers between devices  12.2 us (34%)
  waiting for transfers between devices  8.82 us (25%)
  other arithmetic  0.89 us (2%)
  local copies, waits for them, and re-layouts  0.74 us (2%)
    pallas_call x7, Pallas kernels, run_kernel(): pl.pallas_call(kernel, out_shape=out_shape, in_specs=specs, out_specs=tup...  12.5 us
    ppermute x3, starting transfers between devices, on_device(): lax.ppermute(line, 'gx', exchange_pairs(rows, s))  4.45 us
    ppermute x3, starting transfers between devices, on_device(): lax.ppermute(part, 'gx', return_pairs(rows, s))  4.45 us
    ppermute x3, waiting for transfers between devices, on_device(): lax.ppermute(part, 'gx', return_pairs(rows, s))  3.5 us
    ppermute x1, starting transfers between devices, on_device(): lax.ppermute(block, 'gy', exchange_pairs(columns, s))  3.06 us
    ppermute x3, waiting for transfers between devices, on_device(): lax.ppermute(line, 'gx', exchange_pairs(rows, s))  2.81 us
    ppermute x1, waiting for transfers between devices, on_device(): got = lax.ppermute(send, 'gz', exchange_pairs(levels, 1))  1.36 us
    ppermute x1, waiting for transfers between devices, on_device(): other = lax.ppermute(own, 'gz', exchange_pairs(levels, 1))  1.15 us
  transfers between devices with their start and end apart: 9, of which 6 were waited for; matrix products, arithmetic and copies ran while one was open for 0% of the time, Pallas kernels for 14%

profile of v2, /device:TPU:0, one launch (start us, length us, event | category | flops | bytes accessed | tf_op | source)
XLA Modules:
  0.0 35.3 jit_solution(15953447298450621907)
XLA Ops:
  0.0 0.0 copy-start.7
  0.0 0.0 copy-start.5
  0.0 0.0 copy-start.6
  0.0 0.0 copy-start
  0.0 0.8 %fusion.4 = (s32[1024]{0:T(1024)S(1)}, s32[1024]{0:T(1024)S(1)}, s32[1024]{0:T(1024)S(1)}) fusion(s32[1024]{0:T(1024)} %param.14, s32[1024]{0:T(1024)} %param.13, s32[]{:T(128)S(6)} %mul.25), kind=kLoop, calls=%fused_computation.23 | loop fusion | flops 65536 | bytes 20484 | tf_op jit(solution)/shard_map/add | solution.py:419
  0.8 0.0 copy-done.7
  0.8 0.0 copy-done.5
  0.8 0.0 copy-done.6
  0.8 0.0 copy-start.1
  0.9 3.1 %collective-permute-start = (f32[8,1024]{1,0:T(8,128)S(1)}, f32[8,1024]{1,0:T(8,128)S(1)}, u32[]{:S(2)}, u32[]{:S(2)}) collective-permute-start(f32[8,1024]{1,0:T(8,128)S(1)} %pad_maximum_fusion.refs_3_), channel_id=1, source_target_pairs={{0,2},{2,0},{1,3},{3,1},{4,6},{6,4},{5,7},{7,5},{8,10},{10,8},{9,1... | collective-permute-start | bytes 98312 | tf_op jit(solution)/shard_map/ppermute | solution.py:434
  3.9 0.1 add_convert_fusion.1.refs_0_.place
  4.0 0.0 copy-start.4
  4.0 0.0 copy-start.2
  4.0 0.0 copy-start.3
  4.0 0.0 copy-done
  4.0 0.0 copy-done.1
  4.0 0.6 %copy-done.4 = f32[16]{0:T(128)S(1)} copy-done((f32[16]{0:T(128)S(1)}, f32[16]{0:T(128)}, u32[]{:S(2)}) %copy-start.4) | copy-done | bytes 88
  4.7 0.0 copy-done.2
  4.7 0.0 copy-done.3
  4.7 2.2 %prepare.1 = (bf16[128,192]{1,0:T(8,128)(2,1)S(1)}, bf16[384,256]{1,0:T(8,128)(2,1)S(1)}, f32[128,128]{1,0:T(8,128)S(1)}, f32[128,128]{1,0:T(8,128)S(1)}, bf16[96,512]{1,0:T(8,128)(2,1)S(1)}) custom-call(bf16[27,4,16]{2,1,0:T(4,128)(2,1)S(1)} %bitcast.15, bf16[27,16,16]{2,1,0:T(8,128)(2,1)S(1)} %bitcast.14, f32[1,16]{1,0:T(1,128)S(1)} %bitcast.16, ...), custom_call_target="tpu_custom_call" | custom-call | flops 1000000 | bytes 492640 | tf_op jit(solution)/shard_map/prepare/pallas_call | solution.py:91
  6.9 0.0 collective-permute-done
  6.9 3.7 %collective-permute-start.3 = (f32[16,1024]{1,0:T(8,128)S(1)}, f32[16,1024]{1,0:T(8,128)S(1)}, u32[]{:S(2)}, u32[]{:S(2)}) collective-permute-start(f32[16,1024]{1,0:T(8,128)S(1)} %concatenate.8.refs_1_), channel_id=1, source_target_pairs={{0,12},{4,8},{8,4},{12,0},{1,13},{5,9},{9,5},{13,1},{2,14},{6,10},... | collective-permute-start | bytes 196616 | tf_op jit(solution)/shard_map/ppermute | solution.py:437
  10.6 0.0 collective-permute-start.2
  10.6 0.8 %collective-permute-start.1 = (f32[16,1024]{1,0:T(8,128)S(1)}, f32[16,1024]{1,0:T(8,128)S(1)}, u32[]{:S(2)}, u32[]{:S(2)}) collective-permute-start(f32[16,1024]{1,0:T(8,128)S(1)} %concatenate.8.refs_1_), channel_id=1, source_target_pairs={{0,4},{4,0},{8,12},{12,8},{1,5},{5,1},{9,13},{13,9},{2,6},{6,2},{1... | collective-permute-start | bytes 196616 | tf_op jit(solution)/shard_map/ppermute | solution.py:437
  11.4 1.8 %paint.2.refs_4_ = f32[240,256]{1,0:T(8,128)S(1)} custom-call(f32[2]{0:T(128)S(1)} %add_convert_fusion.1.refs_0_.place, f32[16,1024]{1,0:T(8,128)S(1)} %concatenate.8.refs_1_), custom_call_target="tpu_custom_call" | custom-call | flops 754974720 | bytes 311304 | tf_op jit(solution)/shard_map/paint/pallas_call | solution.py:91
  13.2 0.6 %collective-permute-done.3.refs_3_.refs_5_ = f32[16,1024]{1,0:T(8,128)S(1)} collective-permute-done((f32[16,1024]{1,0:T(8,128)S(1)}, f32[16,1024]{1,0:T(8,128)S(1)}, u32[]{:S(2)}, u32[]{:S(2)}) %collective-permute-start.3) | collective-permute-done | bytes 65568 | tf_op jit(solution)/shard_map/ppermute | solution.py:437
  13.9 2.2 %collective-permute-done.2.refs_2_.refs_4_ = f32[16,1024]{1,0:T(8,128)S(1)} collective-permute-done((f32[16,1024]{1,0:T(8,128)S(1)}, f32[16,1024]{1,0:T(8,128)S(1)}, u32[]{:S(2)}, u32[]{:S(2)}) %collective-permute-start.2) | collective-permute-done | bytes 65568 | tf_op jit(solution)/shard_map/ppermute | solution.py:437
  16.0 0.0 collective-permute-done.1.refs_1_.refs_3_
  16.0 4.4 %paint.3 = (f32[144,256]{1,0:T(8,128)S(1)}, f32[144,256]{1,0:T(8,128)S(1)}) custom-call(f32[2]{0:T(128)S(1)} %add_convert_fusion.1.refs_0_.place, f32[16,1024]{1,0:T(8,128)S(1)} %collective-permute-done.1.refs_1_.refs_3_, f32[16,1024]{1,0:T(8,128)S(1)} %collective-permute-done.2.refs_2_.refs_4_, f32[16,1024]{1,0:T(8,128)S(1)} %collective-permute-done.3.refs_3_.refs_5_, ...), custom_call_target="tpu_custom_call" | custom-call | flops 2264924160 | bytes 802824 | tf_op jit(solution)/shard_map/paint/pallas_call | solution.py:91
  20.4 0.1 collective-permute-start.4
  20.5 1.4 %collective-permute-done.4.got = f32[144,256]{1,0:T(8,128)S(1)} collective-permute-done((f32[144,256]{1,0:T(8,128)S(1)}, f32[144,256]{1,0:T(8,128)S(1)}, u32[]{:S(2)}, u32[]{:S(2)}) %collective-permute-start.4) | collective-permute-done | bytes 147488 | tf_op jit(solution)/shard_map/ppermute | solution.py:441
  21.9 1.6 %mesh_step.1.refs_1_ = f32[96,256]{1,0:T(8,128)S(1)} custom-call(f32[2]{0:T(128)S(1)} %add_convert_fusion.1.refs_0_.place, f32[144,256]{1,0:T(8,128)S(1)} %get-tuple-element.16.keep, f32[144,256]{1,0:T(8,128)S(1)} %collective-permute-done.4.got, bf16[128,192]{1,0:T(8,128)(2,1)S(1)} %get-tuple-element.18.w1, bf16[384,256]{1,0:T(8,128)(2,1)S(1)} %get-tuple-element.19.w2, ...), custom_call_target="tpu_custom_call" | custom-call | flops 200000000 | bytes 868360 | tf_op jit(solution)/shard_map/mesh_step/pallas_call | solution.py:91
  23.5 0.2 collective-permute-start.5
  23.7 1.2 %collective-permute-done.5.refs_2_ = f32[96,256]{1,0:T(8,128)S(1)} collective-permute-done((f32[96,256]{1,0:T(8,128)S(1)}, f32[96,256]{1,0:T(8,128)S(1)}, u32[]{:S(2)}, u32[]{:S(2)}) %collective-permute-start.5) | collective-permute-done | bytes 98336 | tf_op jit(solution)/shard_map/ppermute | solution.py:443
  24.8 1.1 %sample.3 = (f32[3,1024]{1,0:T(4,128)S(1)}, f32[3,1024]{1,0:T(4,128)S(1)}, f32[3,1024]{1,0:T(4,128)S(1)}) custom-call(f32[2]{0:T(128)S(1)} %add_convert_fusion.1.refs_0_.place, f32[96,256]{1,0:T(8,128)S(1)} %mesh_step.1.refs_1_, f32[96,256]{1,0:T(8,128)S(1)} %collective-permute-done.5.refs_2_, f32[16,1024]{1,0:T(8,128)S(1)} %collective-permute-done.1.refs_1_.refs_3_, ...), custom_call_target="tpu_custom_call" | custom-call | flops 226492416 | bytes 430088 | tf_op jit(solution)/shard_map/sample/pallas_call | solution.py:91
  26.0 1.0 %collective-permute-start.6 = (f32[3,1024]{1,0:T(4,128)S(1)}, f32[3,1024]{1,0:T(4,128)S(1)}, u32[]{:S(2)}, u32[]{:S(2)}) collective-permute-start(f32[3,1024]{1,0:T(4,128)S(1)} %get-tuple-element.22), channel_id=1, source_target_pairs={{4,0},{0,4},{12,8},{8,12},{5,1},{1,5},{13,9},{9,13},{6,2},{2,6},{1... | collective-permute-start | bytes 36872 | tf_op jit(solution)/shard_map/ppermute | solution.py:446
  27.0 2.2 %collective-permute-start.7 = (f32[3,1024]{1,0:T(4,128)S(1)}, f32[3,1024]{1,0:T(4,128)S(1)}, u32[]{:S(2)}, u32[]{:S(2)}) collective-permute-start(f32[3,1024]{1,0:T(4,128)S(1)} %get-tuple-element.23), channel_id=1, source_target_pairs={{8,0},{12,4},{0,8},{4,12},{9,1},{13,5},{1,9},{5,13},{10,2},{14,6},... | collective-permute-start | bytes 36872 | tf_op jit(solution)/shard_map/ppermute | solution.py:446
  29.2 1.2 %collective-permute-start.8 = (f32[3,1024]{1,0:T(4,128)S(1)}, f32[3,1024]{1,0:T(4,128)S(1)}, u32[]{:S(2)}, u32[]{:S(2)}) collective-permute-start(f32[3,1024]{1,0:T(4,128)S(1)} %get-tuple-element.24), channel_id=1, source_target_pairs={{12,0},{8,4},{4,8},{0,12},{13,1},{9,5},{5,9},{1,13},{14,2},{10,6},... | collective-permute-start | bytes 36872 | tf_op jit(solution)/shard_map/ppermute | solution.py:446
  30.4 0.8 %sample.2.refs_0_ = f32[3,1024]{1,0:T(4,128)S(1)} custom-call(f32[2]{0:T(128)S(1)} %add_convert_fusion.1.refs_0_.place, f32[96,256]{1,0:T(8,128)S(1)} %mesh_step.1.refs_1_, f32[96,256]{1,0:T(8,128)S(1)} %collective-permute-done.5.refs_2_, f32[8,1024]{1,0:T(8,128)S(1)} %pad_maximum_fusion.refs_3_), custom_call_target="tpu_custom_call" | custom-call | flops 75497472 | bytes 241672 | tf_op jit(solution)/shard_map/sample/pallas_call | solution.py:91
  31.2 0.0 collective-permute-done.6.refs_1_
  31.2 0.5 %collective-permute-done.7.refs_2_ = f32[3,1024]{1,0:T(4,128)S(1)} collective-permute-done((f32[3,1024]{1,0:T(4,128)S(1)}, f32[3,1024]{1,0:T(4,128)S(1)}, u32[]{:S(2)}, u32[]{:S(2)}) %collective-permute-start.7) | collective-permute-done | bytes 12320 | tf_op jit(solution)/shard_map/ppermute | solution.py:446
  31.8 3.0 %collective-permute-done.8.refs_3_ = f32[3,1024]{1,0:T(4,128)S(1)} collective-permute-done((f32[3,1024]{1,0:T(4,128)S(1)}, f32[3,1024]{1,0:T(4,128)S(1)}, u32[]{:S(2)}, u32[]{:S(2)}) %collective-permute-start.8) | collective-permute-done | bytes 12320 | tf_op jit(solution)/shard_map/ppermute | solution.py:446
  34.7 0.6 %finish.1 = f32[3,1024]{1,0:T(4,128)} custom-call(f32[3,1024]{1,0:T(4,128)S(1)} %sample.2.refs_0_, f32[3,1024]{1,0:T(4,128)S(1)} %collective-permute-done.6.refs_1_, f32[3,1024]{1,0:T(4,128)S(1)} %collective-permute-done.7.refs_2_, f32[3,1024]{1,0:T(4,128)S(1)} %collective-permute-done.8.refs_3_), custom_call_target="tpu_custom_call" | custom-call | bytes 61440 | tf_op jit(solution)/shard_map/finish/pallas_call | solution.py:91
  (4 shorter events, 0.1 us)
Async XLA Ops:
  0.0 0.8 %copy-start.7 = (f32[3,1024]{1,0:T(4,128)S(1)}, f32[3,1024]{1,0:T(4,128)}, u32[]{:S(2)}) copy-start(f32[3,1024]{1,0:T(4,128)} %param.12) | copy-start | bytes 36868
  0.0 0.8 %copy-start.5 = (f32[1024]{0:T(1024)S(1)}, f32[1024]{0:T(1024)}, u32[]{:S(2)}) copy-start(f32[1024]{0:T(1024)} %param.11) | copy-start | bytes 12292
  0.0 0.8 %copy-start.6 = (f32[3,1024]{1,0:T(4,128)S(1)}, f32[3,1024]{1,0:T(4,128)}, u32[]{:S(2)}) copy-start(f32[3,1024]{1,0:T(4,128)} %param.10) | copy-start | bytes 36868
  0.0 4.0 %copy-start = (bf16[16,16,3,3,3]{1,0,4,3,2:T(8,128)(2,1)S(1)}, bf16[16,16,3,3,3]{1,0,4,3,2:T(8,128)(2,1)}, u32[]{:S(2)}) copy-start(bf16[16,16,3,3,3]{1,0,4,3,2:T(8,128)(2,1)} %param.17) | copy-start | bytes 41476
  0.8 3.2 %copy-start.1 = (bf16[16,4,3,3,3]{0,1,4,3,2:T(4,128)(2,1)S(1)}, bf16[16,4,3,3,3]{0,1,4,3,2:T(4,128)(2,1)}, u32[]{:S(2)}) copy-start(bf16[16,4,3,3,3]{0,1,4,3,2:T(4,128)(2,1)} %param.15) | copy-start | bytes 10372
  0.9 6.0 %collective-permute-start = (f32[8,1024]{1,0:T(8,128)S(1)}, f32[8,1024]{1,0:T(8,128)S(1)}, u32[]{:S(2)}, u32[]{:S(2)}) collective-permute-start(f32[8,1024]{1,0:T(8,128)S(1)} %pad_maximum_fusion.refs_3_), channel_id=1, source_target_pairs={{0,2},{2,0},{1,3},{3,1},{4,6},{6,4},{5,7},{7,5},{8,10},{10,8},{9,1... | collective-permute-start | bytes 98312 | tf_op jit(solution)/shard_map/ppermute | solution.py:434
  4.0 0.7 %copy-start.4 = (f32[16]{0:T(128)S(1)}, f32[16]{0:T(128)}, u32[]{:S(2)}) copy-start(f32[16]{0:T(128)} %param.18) | copy-start | bytes 196
  4.0 0.7 %copy-start.2 = (bf16[3,16]{1,0:T(4,128)(2,1)S(1)}, bf16[3,16]{1,0:T(4,128)(2,1)}, u32[]{:S(2)}) copy-start(bf16[3,16]{1,0:T(4,128)(2,1)} %hw_ref.1) | copy-start | bytes 292
  4.0 0.7 %copy-start.3 = (f32[16]{0:T(128)S(1)}, f32[16]{0:T(128)}, u32[]{:S(2)}) copy-start(f32[16]{0:T(128)} %param.16) | copy-start | bytes 196
  6.9 6.9 %collective-permute-start.3 = (f32[16,1024]{1,0:T(8,128)S(1)}, f32[16,1024]{1,0:T(8,128)S(1)}, u32[]{:S(2)}, u32[]{:S(2)}) collective-permute-start(f32[16,1024]{1,0:T(8,128)S(1)} %concatenate.8.refs_1_), channel_id=1, source_target_pairs={{0,12},{4,8},{8,4},{12,0},{1,13},{5,9},{9,5},{13,1},{2,14},{6,10},... | collective-permute-start | bytes 196616 | tf_op jit(solution)/shard_map/ppermute | solution.py:437
  10.6 5.4 %collective-permute-start.2 = (f32[16,1024]{1,0:T(8,128)S(1)}, f32[16,1024]{1,0:T(8,128)S(1)}, u32[]{:S(2)}, u32[]{:S(2)}) collective-permute-start(f32[16,1024]{1,0:T(8,128)S(1)} %concatenate.8.refs_1_), channel_id=1, source_target_pairs={{0,8},{4,12},{8,0},{12,4},{1,9},{5,13},{9,1},{13,5},{2,10},{6,14},... | collective-permute-start | bytes 196616 | tf_op jit(solution)/shard_map/ppermute | solution.py:437
  10.6 5.4 %collective-permute-start.1 = (f32[16,1024]{1,0:T(8,128)S(1)}, f32[16,1024]{1,0:T(8,128)S(1)}, u32[]{:S(2)}, u32[]{:S(2)}) collective-permute-start(f32[16,1024]{1,0:T(8,128)S(1)} %concatenate.8.refs_1_), channel_id=1, source_target_pairs={{0,4},{4,0},{8,12},{12,8},{1,5},{5,1},{9,13},{13,9},{2,6},{6,2},{1... | collective-permute-start | bytes 196616 | tf_op jit(solution)/shard_map/ppermute | solution.py:437
  20.4 1.4 %collective-permute-start.4 = (f32[144,256]{1,0:T(8,128)S(1)}, f32[144,256]{1,0:T(8,128)S(1)}, u32[]{:S(2)}, u32[]{:S(2)}) collective-permute-start(f32[144,256]{1,0:T(8,128)S(1)} %get-tuple-element.17), channel_id=1, source_target_pairs={{0,1},{1,0},{2,3},{3,2},{4,5},{5,4},{6,7},{7,6},{8,9},{9,8},{10,11... | collective-permute-start | bytes 442376 | tf_op jit(solution)/shard_map/ppermute | solution.py:441
  23.5 1.4 %collective-permute-start.5 = (f32[96,256]{1,0:T(8,128)S(1)}, f32[96,256]{1,0:T(8,128)S(1)}, u32[]{:S(2)}, u32[]{:S(2)}) collective-permute-start(f32[96,256]{1,0:T(8,128)S(1)} %mesh_step.1.refs_1_), channel_id=1, source_target_pairs={{0,1},{1,0},{2,3},{3,2},{4,5},{5,4},{6,7},{7,6},{8,9},{9,8},{10,11... | collective-permute-start | bytes 294920 | tf_op jit(solution)/shard_map/ppermute | solution.py:443
  26.0 5.3 %collective-permute-start.6 = (f32[3,1024]{1,0:T(4,128)S(1)}, f32[3,1024]{1,0:T(4,128)S(1)}, u32[]{:S(2)}, u32[]{:S(2)}) collective-permute-start(f32[3,1024]{1,0:T(4,128)S(1)} %get-tuple-element.22), channel_id=1, source_target_pairs={{4,0},{0,4},{12,8},{8,12},{5,1},{1,5},{13,9},{9,13},{6,2},{2,6},{1... | collective-permute-start | bytes 36872 | tf_op jit(solution)/shard_map/ppermute | solution.py:446
  27.0 4.8 %collective-permute-start.7 = (f32[3,1024]{1,0:T(4,128)S(1)}, f32[3,1024]{1,0:T(4,128)S(1)}, u32[]{:S(2)}, u32[]{:S(2)}) collective-permute-start(f32[3,1024]{1,0:T(4,128)S(1)} %get-tuple-element.23), channel_id=1, source_target_pairs={{8,0},{12,4},{0,8},{4,12},{9,1},{13,5},{1,9},{5,13},{10,2},{14,6},... | collective-permute-start | bytes 36872 | tf_op jit(solution)/shard_map/ppermute | solution.py:446
  29.2 5.5 %collective-permute-start.8 = (f32[3,1024]{1,0:T(4,128)S(1)}, f32[3,1024]{1,0:T(4,128)S(1)}, u32[]{:S(2)}, u32[]{:S(2)}) collective-permute-start(f32[3,1024]{1,0:T(4,128)S(1)} %get-tuple-element.24), channel_id=1, source_target_pairs={{12,0},{8,4},{4,8},{0,12},{13,1},{9,5},{5,9},{1,13},{14,2},{10,6},... | collective-permute-start | bytes 36872 | tf_op jit(solution)/shard_map/ppermute | solution.py:446
